TPU v7x, 256 devices: a whole 4x4x8 slice. The times are simulated.
256 devices in a mesh: front: 8 (over z), row: 32 (over x, y, core).
Axes of the slice: x: 4, y: 4, z: 8, core: 2. Of those that a mesh axis runs over, the one named last changes fastest.
Arguments:
- panels: bfloat16 [8, 4096, 1280], P('front', 'row'), may hold values from -6 to 6
- reflectors: bfloat16 [8, 4096, 512], P('front', 'row'), may hold values from -6 to 6
- block_coeffs: bfloat16 [8, 512, 512], P('front')
- block_mask: int32 [8, 32, 4], P('front', 'row'), may hold values 0 or 1
- block_starts: int32 [8, 4], P('front'), may hold values from 0 to 2048, as said below
- carry_map: int32 [8, 1024], P('front'), may hold values from 0 to 4095, as said below
Outputs:
- panels_out: bfloat16 [8, 4096, 1280], P('front', 'row')
Inputs may be any that keep to these rules, and one draw needn't show every extreme that they name: `block_starts`: nondecreasing along the reflector blocks of a front. `carry_map`: within a front the targets are distinct, and carried row i lands in the 128-row block number i % 32, which receives exactly 32 carried rows, its last row among them.
All inputs are finite; a program needn't handle non-finite values. No bound on the sum of `block_mask` on one device may be relied on, other than what follows from the above.
Results may differ from a plain program's by a relative error of at most 0.017.
Values may be sent and summed in bfloat16 or wider, within the bound.
No kernel may reach another device: no remote copies, remote signals or barrier semaphores. Data moves between devices by JAX's collectives and lax.ppermute only.
A program may use at most 64 MiB of HBM per device.

v0:
```python
import jax
import jax.numpy as jnp
from jax import lax
from jax.experimental import pallas as pl
from jax.experimental.pallas import tpu as pltpu
from jax.sharding import PartitionSpec as P


BF = jnp.bfloat16
F32 = jnp.float32
I32 = jnp.int32
SIDE = 4
ROWS = 32
SPAN = 128
EACH = 32
CARRIED = ROWS * EACH
TAIL = 24
WIDTH = 512


def mm(a, b, dims=((1,), (0,))):
    return lax.dot_general(a, b, (dims, ((), ())), preferred_element_type=F32)


def place(x, y, core):
    return ((x % SIDE) * SIDE + y % SIDE) * 2 + core


def shift(second, step):
    pairs = []
    for x in range(SIDE):
        for y in range(SIDE):
            for core in range(2):
                along_x = (core == 0) != second
                pairs.append((place(x, y, core), place(x + step * along_x, y + step * (not along_x), core)))
    return pairs


SWAP = [(place(x, y, c), place(x, y, 1 - c)) for x in range(SIDE) for y in range(SIDE) for c in range(2)]

VMEM = pl.BlockSpec(memory_space=pltpu.VMEM)
SMEM = pl.BlockSpec(memory_space=pltpu.SMEM)
HBM = pl.BlockSpec(memory_space=pltpu.HBM)


def call(kernel, outs, specs, limit=20, scratch=(), cost=None):
    return pl.pallas_call(
        kernel,
        out_shape=outs,
        in_specs=specs,
        out_specs=jax.tree.map(lambda _: VMEM, outs),
        scratch_shapes=scratch,
        compiler_params=pltpu.CompilerParams(vmem_limit_bytes=limit << 20),
        cost_estimate=cost,
    )


def shape(dims, dtype=BF):
    return jax.ShapeDtypeStruct(dims, dtype)


def mask_kernel(row, mask, starts, refl, own, mask_s, starts_s, refl_v, sems):
    moves = [
        pltpu.make_async_copy(source, target, sems.at[i])
        for i, (source, target) in enumerate(((refl, refl_v), (mask, mask_s), (starts, starts_s)))
    ]
    for move in moves:
        move.start()
    for move in moves:
        move.wait()
    ids = row[0] * SPAN + lax.broadcasted_iota(I32, (SPAN, 128), 0)
    for k in range(WIDTH // 128):
        kept = (ids >= starts_s[0, k]) & (mask_s[0, 0, k] == 1)
        part = refl_v[0, :, k * 128 : (k + 1) * 128].astype(F32)
        own[:, k * 128 : (k + 1) * 128] = jnp.where(kept, part, 0.0).astype(BF)


def turn_kernel(panels, out):
    for k in range(panels.shape[2] // 128):
        part = panels[0, :, k * 128 : (k + 1) * 128]
        out[k * 128 : (k + 1) * 128, :] = part.T


def slots(row, sibling):
    x, y, core = row // (2 * SIDE), (row // 2) % SIDE, row % 2
    who = 1 - core if sibling else core
    for j in range(SIDE):
        for k in range(SIDE):
            dx = jnp.where(who == 0, k, j)
            dy = jnp.where(who == 0, j, k)
            yield j, k, (((x + dx) % SIDE) * SIDE + (y + dy) % SIDE) * 2 + who


def base_kernel(row, *refs):
    mine, theirs, (got, coeffs, eff, base, first, sent) = refs[:8], refs[8:16], refs[16:]
    acc = jnp.zeros(base.shape, F32)
    for sibling, parts in enumerate((mine, theirs)):
        held = None
        for j, k, block in slots(row[0], sibling):
            tile = parts[2 * j + k // 2][k % 2]
            eff[block] = tile
            if held is None:
                held = (got[block], tile)
            else:
                lhs = jnp.concatenate([held[0], got[block]], axis=1)
                acc += mm(lhs, jnp.concatenate([held[1], tile], axis=0))
                held = None
    m = mm(acc.astype(BF), coeffs[0])
    base[...] = m
    m = m.astype(BF)
    for t in range(TAIL, ROWS, 2):
        low = eff[t : t + 2].reshape(2 * SPAN, WIDTH)
        have = jnp.concatenate([got[t], got[t + 1]], axis=1).astype(F32)
        res = have - mm(m, low, ((1,), (1,)))
        at = pl.ds((t - TAIL) * SPAN, 2 * SPAN)
        first[:, at] = res
        sent[:, at] = res.astype(BF)


def hop_kernel(offsets, eff, coeffs, turn, hop, gath, fall):
    lane = lax.broadcasted_iota(I32, (2 * EACH, 2 * SPAN), 1)
    for b in range(0, ROWS, 2):
        where = jnp.concatenate([offsets[:, b : b + 1], offsets[:, b + 1 : b + 2] + SPAN], axis=0)
        pick = (where == lane).astype(F32).astype(BF)
        rows = mm(pick, eff[b : b + 2].reshape(2 * SPAN, WIDTH))
        for h in range(2):
            for k in range(WIDTH // 128):
                tile = rows[h * EACH : (h + 1) * EACH, k * 128 : (k + 1) * 128]
                gath[k, pl.ds(b + h, EACH, stride=ROWS), :] = tile
    for r in range(0, CARRIED, 256):
        wide = jnp.concatenate([gath[k, r : r + 256, :].astype(BF) for k in range(WIDTH // 128)], axis=1)
        turn[r : r + 256, :] = mm(wide, coeffs[0]).astype(BF)
    lane = lax.broadcasted_iota(I32, (EACH, SPAN), 1)
    for t in range(TAIL, ROWS, 2):
        low = eff[t : t + 2].reshape(2 * SPAN, WIDTH)
        for r in range(0, CARRIED, 256):
            down = -mm(turn[r : r + 256, :], low, ((1,), (1,)))
            for h in range(2):
                fall[h, r : r + 256, :] = down[:, h * SPAN : (h + 1) * SPAN]
        for h in range(2):
            pick = (offsets[:, t + h : t + h + 1] == lane).astype(F32)
            at = (h, pl.ds(t + h, EACH, stride=ROWS), slice(None))
            fall[at] = fall[at] + pick
            hop[:, (t + h - TAIL) * SPAN : (t + h - TAIL + 1) * SPAN] = fall[h].astype(BF)


def table_kernel(offsets, order, spread):
    for r in range(0, CARRIED, 128):
        down = r + lax.broadcasted_iota(I32, (128, CARRIED), 0)
        right = lax.broadcasted_iota(I32, (128, CARRIED), 1)
        order[r : r + 128, :] = ((right % EACH) * ROWS + right // EACH == down).astype(F32).astype(BF)
    lane = lax.broadcasted_iota(I32, (EACH, 8 * SPAN), 1)
    for b in range(ROWS):
        where = offsets[:, b : b + 1] + (b % 8) * SPAN
        spread[b * EACH : (b + 1) * EACH, :] = (where == lane).astype(F32).astype(BF)


def last_kernel(c1, c2, c3, c4, c5, c6, c7, base, turn, order, spread, got, eff, out):
    cin = c1[...].astype(F32)
    for c in (c2, c3, c4, c5, c6, c7):
        cin += c[...].astype(F32)
    cin = cin.astype(BF)
    m = (base[...] + mm(cin, turn[...])).astype(BF)
    sorted_in = mm(cin, order[...]).astype(BF)
    for g in range(4):
        moved = mm(sorted_in[:, g * 256 : (g + 1) * 256], spread[g * 256 : (g + 1) * 256, :])
        for p in range(0, 8, 2):
            b = 8 * g + p
            have = jnp.concatenate([got[b], got[b + 1]], axis=1).astype(F32)
            a = (have + moved[:, p * SPAN : (p + 2) * SPAN]).astype(BF).astype(F32)
            back = mm(m, eff[b : b + 2].reshape(2 * SPAN, WIDTH), ((1,), (1,)))
            res = (a - back).astype(BF)
            out[b] = res[:, :SPAN]
            out[b + 1] = res[:, SPAN:]


def gather_rows(own):
    pp = lambda value, pairs: lax.ppermute(value, "row", pairs)
    half = own.shape[0] // 2
    right = pp(own, shift(False, -1))
    left = pp(own, shift(False, 1))
    far_a = pp(left[:half], shift(False, 1))
    far_b = pp(right[half:], shift(False, -1))
    near = jnp.stack([own, right])
    near_left = pp(near, shift(True, 1))
    near_right = pp(near, shift(True, -1))
    rest = jnp.stack([jnp.concatenate([far_a, far_b]), left])
    rest_right = pp(rest, shift(True, -1))
    rest_left = pp(rest, shift(True, 1))
    near_far = pp(near_left, shift(True, 1))
    rest_far = pp(rest_right, shift(True, -1))
    mine = [near, rest, near_right, rest_right, near_far, rest_far, near_left, rest_left]
    theirs = [pp(value, SWAP) for value in mine]
    return mine + theirs


def work(panels, reflectors, block_coeffs, block_mask, block_starts, carry_map):
    fronts = lax.axis_size("front")
    row = lax.axis_index("row").reshape(1)
    cols = panels.shape[2]
    part = cols // ROWS

    pieces = call(turn_kernel, shape((cols, SPAN)), [VMEM])(panels)
    own = call(
        mask_kernel,
        shape((SPAN, WIDTH)),
        [SMEM] + [HBM] * 3,
        scratch=[
            pltpu.SMEM(block_mask.shape, I32),
            pltpu.SMEM(block_starts.shape, I32),
            pltpu.VMEM(reflectors.shape, BF),
            pltpu.SemaphoreType.DMA((3,)),
        ],
    )(row, block_mask, block_starts, reflectors)
    got = lax.all_to_all(pieces.reshape(ROWS, part, SPAN), "row", 0, 0, tiled=True)
    parts = gather_rows(own)

    offsets = carry_map[0].reshape(EACH, ROWS) - SPAN * jnp.arange(ROWS, dtype=I32)
    order, spread = call(table_kernel, (shape((CARRIED, CARRIED)), shape((CARRIED, 8 * SPAN))), [VMEM])(offsets)

    eff, base, first, sent = call(
        base_kernel,
        (
            shape((ROWS, SPAN, WIDTH)),
            shape((part, WIDTH), F32),
            shape((part, CARRIED), F32),
            shape((part, CARRIED)),
        ),
        [SMEM] + [VMEM] * 18,
    )(row, *parts, got, block_coeffs)

    came = [lax.ppermute(sent, "front", [(0, 1)])]
    turn, hop = call(
        hop_kernel,
        (shape((CARRIED, WIDTH)), shape((CARRIED, CARRIED))),
        [VMEM] * 3,
        scratch=[pltpu.VMEM((WIDTH // 128, CARRIED, 128), F32), pltpu.VMEM((2, CARRIED, SPAN), F32)],
    )(offsets, eff, block_coeffs)
    for step in range(2, fronts):
        sent = (first + mm(came[-1], hop)).astype(BF)
        came.append(lax.ppermute(sent, "front", [(step - 1, step)]))

    none = [jnp.zeros_like(sent)] * (7 - len(came))
    out = call(last_kernel, shape((ROWS, part, SPAN)), [VMEM] * 13)(*came, *none, base, turn, order, spread, got, eff)
    home = lax.all_to_all(out, "row", 0, 0, tiled=True)
    return home.reshape(cols, SPAN).T[None]


def solution(mesh):
    in_specs = (
        P("front", "row", None),
        P("front", "row", None),
        P("front", None, None),
        P("front", "row", None),
        P("front", None),
        P("front", None),
    )
    out_specs = P("front", "row", None)
    return jax.shard_map(work, mesh=mesh, in_specs=in_specs, out_specs=out_specs, check_vma=False)
```

profile of v0, /device:TPU:225, one launch (start us, length us, event | category | flops | bytes accessed | tf_op | source)
XLA Modules:
  0.0 97.9 jit_solution(6216882798186062176)
XLA Ops:
  0.0 1.0 copy-done.2
  3.1 1.4 %collective-permute-start.1 = (bf16[128,512]{1,0:T(8,128)(2,1)S(1)}, bf16[128,512]{1,0:T(8,128)(2,1)S(1)}, u32[]{:S(2)}, u32[]{:S(2)}) collective-permute-start(bf16[128,512]{1,0:T(8,128)(2,1)S(1)} %shard_map.64), channel_id=1, source_target_pairs={{0,8},{1,3},{2,10},{3,5},{4,12},{5,7},{6,14},{7,1},{8,16},{9,11},{... | collective-permute-start | bytes 393224 | tf_op jit(solution)/shard_map/ppermute | solution.py:178
  4.4 1.5 %collective-permute-start = (bf16[128,512]{1,0:T(8,128)(2,1)S(1)}, bf16[128,512]{1,0:T(8,128)(2,1)S(1)}, u32[]{:S(2)}, u32[]{:S(2)}) collective-permute-start(bf16[128,512]{1,0:T(8,128)(2,1)S(1)} %shard_map.64), channel_id=1, source_target_pairs={{0,24},{1,7},{2,26},{3,1},{4,28},{5,3},{6,30},{7,5},{8,0},{9,15},{... | collective-permute-start | bytes 393224 | tf_op jit(solution)/shard_map/ppermute | solution.py:178
  6.0 2.6 %collective-permute-done.1 = bf16[128,512]{1,0:T(8,128)(2,1)S(1)} collective-permute-done((bf16[128,512]{1,0:T(8,128)(2,1)S(1)}, bf16[128,512]{1,0:T(8,128)(2,1)S(1)}, u32[]{:S(2)}, u32[]{:S(2)}) %collective-permute-start.1) | collective-permute-done | bytes 131104 | tf_op jit(solution)/shard_map/ppermute | solution.py:178
  8.6 2.7 %collective-permute-start.3 = (bf16[64,512]{1,0:T(8,128)(2,1)S(1)}, bf16[64,512]{1,0:T(8,128)(2,1)S(1)}, u32[]{:S(2)}, u32[]{:S(2)}) collective-permute-start(bf16[64,512]{1,0:T(8,128)(2,1)S(1)} %slice.9), channel_id=1, source_target_pairs={{0,24},{1,7},{2,26},{3,1},{4,28},{5,3},{6,30},{7,5},{8,0},{9,15},{... | collective-permute-start | bytes 196616 | tf_op jit(solution)/shard_map/ppermute | solution.py:178
  11.3 2.1 %collective-permute-start.10 = (bf16[2,128,512]{2,1,0:T(8,128)(2,1)S(1)}, bf16[2,128,512]{2,1,0:T(8,128)(2,1)S(1)}, u32[]{:S(2)}, u32[]{:S(2)}) collective-permute-start(bf16[2,128,512]{2,1,0:T(8,128)(2,1)S(1)} %pad_maximum_fusion.refs_0_), channel_id=1, source_target_pairs={{0,1},{1,0},{2,3},{3,2},{4,5},{5,4},{6,7},{7,6},{8,9},{9,8},{10,11... | collective-permute-start | bytes 786440 | tf_op jit(solution)/shard_map/ppermute | solution.py:178
  13.4 2.7 %collective-permute-start.4 = (bf16[2,128,512]{2,1,0:T(8,128)(2,1)S(1)}, bf16[2,128,512]{2,1,0:T(8,128)(2,1)S(1)}, u32[]{:S(2)}, u32[]{:S(2)}) collective-permute-start(bf16[2,128,512]{2,1,0:T(8,128)(2,1)S(1)} %pad_maximum_fusion.refs_0_), channel_id=1, source_target_pairs={{0,6},{1,25},{2,0},{3,27},{4,2},{5,29},{6,4},{7,31},{8,14},{9,1},{... | collective-permute-start | bytes 786440 | tf_op jit(solution)/shard_map/ppermute | solution.py:178
  16.3 2.4 %collective-permute-start.11 = (bf16[2,128,512]{2,1,0:T(8,128)(2,1)S(1)}, bf16[2,128,512]{2,1,0:T(8,128)(2,1)S(1)}, u32[]{:S(2)}, u32[]{:S(2)}) collective-permute-start(bf16[2,128,512]{2,1,0:T(8,128)(2,1)S(1)} %pad_maximum_fusion.1.refs_1_), channel_id=1, source_target_pairs={{0,1},{1,0},{2,3},{3,2},{4,5},{5,4},{6,7},{7,6},{8,9},{9,8},{10,11... | collective-permute-start | bytes 786440 | tf_op jit(solution)/shard_map/ppermute | solution.py:178
  19.0 1.2 %collective-permute-done.6.refs_6_ = bf16[2,128,512]{2,1,0:T(8,128)(2,1)S(1)} collective-permute-done((bf16[2,128,512]{2,1,0:T(8,128)(2,1)S(1)}, bf16[2,128,512]{2,1,0:T(8,128)(2,1)S(1)}, u32[]{:S(2)}, u32[]{:S(2)}) %collective-permute-start.6) | collective-permute-done | bytes 262176 | tf_op jit(solution)/shard_map/ppermute | solution.py:178
  20.2 0.9 collective-permute-start.16
  21.1 1.1 %collective-permute-done.5.refs_3_ = bf16[2,128,512]{2,1,0:T(8,128)(2,1)S(1)} collective-permute-done((bf16[2,128,512]{2,1,0:T(8,128)(2,1)S(1)}, bf16[2,128,512]{2,1,0:T(8,128)(2,1)S(1)}, u32[]{:S(2)}, u32[]{:S(2)}) %collective-permute-start.5) | collective-permute-done | bytes 262176 | tf_op jit(solution)/shard_map/ppermute | solution.py:178
  22.2 3.1 %collective-permute-start.8 = (bf16[2,128,512]{2,1,0:T(8,128)(2,1)S(1)}, bf16[2,128,512]{2,1,0:T(8,128)(2,1)}, u32[]{:S(2)}, u32[]{:S(2)}) collective-permute-start(bf16[2,128,512]{2,1,0:T(8,128)(2,1)S(1)} %collective-permute-done.5.refs_3_), channel_id=1, source_target_pairs={{0,6},{1,25},{2,0},{3,27},{4,2},{5,29},{6,4},{7,31},{8,14},{9,1},{... | collective-permute-start | bytes 786440 | tf_op jit(solution)/shard_map/ppermute | solution.py:178
  25.4 1.0 copy-done.1
  26.3 0.9 shard_map.65
  27.2 5.6 %all-to-all-start = ((bf16[32,40,128]{2,1,0:T(8,128)(2,1)}), bf16[32,40,128]{2,1,0:T(8,128)(2,1)S(1)}, u32[]{:S(2)}, u32[]{:S(2)}) async-start(bf16[32,40,128]{2,1,0:T(8,128)(2,1)} %bitcast.5), calls=%async_computation | async-start | bytes 655360 | tf_op jit(solution)/shard_map/all_to_all | solution.py:215
  35.3 7.1 %all-to-all-done.refs_16_.got = bf16[32,40,128]{2,1,0:T(8,128)(2,1)S(1)} async-done(((bf16[32,40,128]{2,1,0:T(8,128)(2,1)}), bf16[32,40,128]{2,1,0:T(8,128)(2,1)S(1)}, u32[]{:S(2)}, u32[]{:S(2)}) %all-to-all-start) | async-done | bytes 327712 | tf_op jit(solution)/shard_map/all_to_all | solution.py:215
  42.5 2.9 %shard_map.66 = (bf16[32,128,512]{2,1,0:T(8,128)(2,1)S(1)}, f32[40,512]{1,0:T(8,128)S(1)}, f32[40,1024]{1,0:T(8,128)S(1)}, bf16[40,1024]{1,0:T(8,128)(2,1)S(1)}) custom-call(s32[1]{0:T(128)} %bitcast.row, bf16[2,128,512]{2,1,0:T(8,128)(2,1)S(1)} %pad_maximum_fusion.refs_0_, bf16[2,128,512]{2,1,0:T(8,128)(2,1)S(1)} %pad_maximum_fusion.1.refs_1_, ...), custom_call_target="tpu_custom_call" | custom-call | tf_op jit(solution)/shard_map/pallas_call | solution.py:221
  46.0 4.6 %shard_map.67 = (bf16[1024,512]{1,0:T(8,128)(2,1)S(1)}, bf16[1024,1024]{1,0:T(8,128)(2,1)S(1)}) custom-call(s32[32,32]{1,0:T(8,128)S(1)} %broadcast_subtract_fusion.offsets, bf16[32,128,512]{2,1,0:T(8,128)(2,1)S(1)} %get-tuple-element.15.eff, bf16[1,512,512]{2,1,0:T(8,128)(2,1)S(1)} %copy-done), custom_call_target="tpu_custom_call" | custom-call | tf_op jit(solution)/shard_map/pallas_call | solution.py:233
  57.0 1.3 %collective-permute-start.24 = (bf16[40,1024]{1,0:T(8,128)(2,1)S(1)}, bf16[40,1024]{1,0:T(8,128)(2,1)S(1)}, u32[]{:S(2)}, u32[]{:S(2)}) collective-permute-start(bf16[40,1024]{1,0:T(8,128)(2,1)S(1)} %fusion.5), channel_id=1, source_target_pairs={{192,224},{193,225},{194,226},{195,227},{196,228},{197,229},{198,2... | collective-permute-start | bytes 245768 | tf_op jit(solution)/shard_map/ppermute | solution.py:241
  58.3 0.9 shard_map.68
  59.2 17.5 %collective-permute-done.24.c7 = bf16[40,1024]{1,0:T(8,128)(2,1)S(1)} collective-permute-done((bf16[40,1024]{1,0:T(8,128)(2,1)S(1)}, bf16[40,1024]{1,0:T(8,128)(2,1)S(1)}, u32[]{:S(2)}, u32[]{:S(2)}) %collective-permute-start.24) | collective-permute-done | bytes 81952 | tf_op jit(solution)/shard_map/ppermute | solution.py:241
  76.7 2.3 %shard_map.69 = bf16[32,40,128]{2,1,0:T(8,128)(2,1)S(1)} custom-call(bf16[40,1024]{1,0:T(8,128)(2,1)S(1)} %collective-permute-done.18.c1, bf16[40,1024]{1,0:T(8,128)(2,1)S(1)} %collective-permute-done.19.c2, bf16[40,1024]{1,0:T(8,128)(2,1)S(1)} %collective-permute-done.20.c3, bf16[40,1024]{1,0:T(8,128)(2,1)S(1)} %collective-permute-done.21.c4, ...), custom_call_target="tpu_custom_call" | custom-call | tf_op jit(solution)/shard_map/pallas_call | solution.py:244
  79.0 18.0 %all_to_all.10 = bf16[32,40,128]{2,1,0:T(8,128)(2,1)S(1)} all-to-all(bf16[32,40,128]{2,1,0:T(8,128)(2,1)S(1)} %shard_map.69), channel_id=1, replica_groups=mesh['front'=8,'row'=32] {'row'}, dimensions={0} | all-to-all | bytes 655360 | tf_op jit(solution)/shard_map/all_to_all | solution.py:245
  97.0 0.9 copy.7
  (64 shorter events, 12.0 us)
Async XLA Ops:
  3.1 5.5 %collective-permute-start.1 = (bf16[128,512]{1,0:T(8,128)(2,1)S(1)}, bf16[128,512]{1,0:T(8,128)(2,1)S(1)}, u32[]{:S(2)}, u32[]{:S(2)}) collective-permute-start(bf16[128,512]{1,0:T(8,128)(2,1)S(1)} %shard_map.64), channel_id=1, source_target_pairs={{0,8},{1,3},{2,10},{3,5},{4,12},{5,7},{6,14},{7,1},{8,16},{9,11},{... | collective-permute-start | bytes 393224 | tf_op jit(solution)/shard_map/ppermute | solution.py:178
  4.4 4.1 %collective-permute-start = (bf16[128,512]{1,0:T(8,128)(2,1)S(1)}, bf16[128,512]{1,0:T(8,128)(2,1)S(1)}, u32[]{:S(2)}, u32[]{:S(2)}) collective-permute-start(bf16[128,512]{1,0:T(8,128)(2,1)S(1)} %shard_map.64), channel_id=1, source_target_pairs={{0,24},{1,7},{2,26},{3,1},{4,28},{5,3},{6,30},{7,5},{8,0},{9,15},{... | collective-permute-start | bytes 393224 | tf_op jit(solution)/shard_map/ppermute | solution.py:178
  8.5 7.6 %collective-permute-start.2 = (bf16[64,512]{1,0:T(8,128)(2,1)S(1)}, bf16[64,512]{1,0:T(8,128)(2,1)S(1)}, u32[]{:S(2)}, u32[]{:S(2)}) collective-permute-start(bf16[64,512]{1,0:T(8,128)(2,1)S(1)} %slice.8), channel_id=1, source_target_pairs={{0,8},{1,3},{2,10},{3,5},{4,12},{5,7},{6,14},{7,1},{8,16},{9,11},{... | collective-permute-start | bytes 196616 | tf_op jit(solution)/shard_map/ppermute | solution.py:178
  8.6 7.6 %collective-permute-start.3 = (bf16[64,512]{1,0:T(8,128)(2,1)S(1)}, bf16[64,512]{1,0:T(8,128)(2,1)S(1)}, u32[]{:S(2)}, u32[]{:S(2)}) collective-permute-start(bf16[64,512]{1,0:T(8,128)(2,1)S(1)} %slice.9), channel_id=1, source_target_pairs={{0,24},{1,7},{2,26},{3,1},{4,28},{5,3},{6,30},{7,5},{8,0},{9,15},{... | collective-permute-start | bytes 196616 | tf_op jit(solution)/shard_map/ppermute | solution.py:178
  11.3 7.4 %collective-permute-start.10 = (bf16[2,128,512]{2,1,0:T(8,128)(2,1)S(1)}, bf16[2,128,512]{2,1,0:T(8,128)(2,1)S(1)}, u32[]{:S(2)}, u32[]{:S(2)}) collective-permute-start(bf16[2,128,512]{2,1,0:T(8,128)(2,1)S(1)} %pad_maximum_fusion.refs_0_), channel_id=1, source_target_pairs={{0,1},{1,0},{2,3},{3,2},{4,5},{5,4},{6,7},{7,6},{8,9},{9,8},{10,11... | collective-permute-start | bytes 786440 | tf_op jit(solution)/shard_map/ppermute | solution.py:178
  13.4 6.7 %collective-permute-start.6 = (bf16[2,128,512]{2,1,0:T(8,128)(2,1)S(1)}, bf16[2,128,512]{2,1,0:T(8,128)(2,1)S(1)}, u32[]{:S(2)}, u32[]{:S(2)}) collective-permute-start(bf16[2,128,512]{2,1,0:T(8,128)(2,1)S(1)} %pad_maximum_fusion.refs_0_), channel_id=1, source_target_pairs={{0,2},{1,9},{2,4},{3,11},{4,6},{5,13},{6,0},{7,15},{8,10},{9,17},{... | collective-permute-start | bytes 786440 | tf_op jit(solution)/shard_map/ppermute | solution.py:178
  13.4 7.7 %collective-permute-start.4 = (bf16[2,128,512]{2,1,0:T(8,128)(2,1)S(1)}, bf16[2,128,512]{2,1,0:T(8,128)(2,1)S(1)}, u32[]{:S(2)}, u32[]{:S(2)}) collective-permute-start(bf16[2,128,512]{2,1,0:T(8,128)(2,1)S(1)} %pad_maximum_fusion.refs_0_), channel_id=1, source_target_pairs={{0,6},{1,25},{2,0},{3,27},{4,2},{5,29},{6,4},{7,31},{8,14},{9,1},{... | collective-permute-start | bytes 786440 | tf_op jit(solution)/shard_map/ppermute | solution.py:178
  16.2 6.1 %collective-permute-start.5 = (bf16[2,128,512]{2,1,0:T(8,128)(2,1)S(1)}, bf16[2,128,512]{2,1,0:T(8,128)(2,1)S(1)}, u32[]{:S(2)}, u32[]{:S(2)}) collective-permute-start(bf16[2,128,512]{2,1,0:T(8,128)(2,1)S(1)} %pad_maximum_fusion.1.refs_1_), channel_id=1, source_target_pairs={{0,6},{1,25},{2,0},{3,27},{4,2},{5,29},{6,4},{7,31},{8,14},{9,1},{... | collective-permute-start | bytes 786440 | tf_op jit(solution)/shard_map/ppermute | solution.py:178
  16.3 16.5 %collective-permute-start.11 = (bf16[2,128,512]{2,1,0:T(8,128)(2,1)S(1)}, bf16[2,128,512]{2,1,0:T(8,128)(2,1)S(1)}, u32[]{:S(2)}, u32[]{:S(2)}) collective-permute-start(bf16[2,128,512]{2,1,0:T(8,128)(2,1)S(1)} %pad_maximum_fusion.1.refs_1_), channel_id=1, source_target_pairs={{0,1},{1,0},{2,3},{3,2},{4,5},{5,4},{6,7},{7,6},{8,9},{9,8},{10,11... | collective-permute-start | bytes 786440 | tf_op jit(solution)/shard_map/ppermute | solution.py:178
  18.7 14.4 %collective-permute-start.9 = (bf16[2,128,512]{2,1,0:T(8,128)(2,1)S(1)}, bf16[2,128,512]{2,1,0:T(8,128)(2,1)S(1)}, u32[]{:S(2)}, u32[]{:S(2)}) collective-permute-start(bf16[2,128,512]{2,1,0:T(8,128)(2,1)S(1)} %pad_maximum_fusion.1.refs_1_), channel_id=1, source_target_pairs={{0,2},{1,9},{2,4},{3,11},{4,6},{5,13},{6,0},{7,15},{8,10},{9,17},{... | collective-permute-start | bytes 786440 | tf_op jit(solution)/shard_map/ppermute | solution.py:178
  20.2 13.2 %collective-permute-start.16 = (bf16[2,128,512]{2,1,0:T(8,128)(2,1)S(1)}, bf16[2,128,512]{2,1,0:T(8,128)(2,1)S(1)}, u32[]{:S(2)}, u32[]{:S(2)}) collective-permute-start(bf16[2,128,512]{2,1,0:T(8,128)(2,1)S(1)} %collective-permute-done.6.refs_6_), channel_id=1, source_target_pairs={{0,1},{1,0},{2,3},{3,2},{4,5},{5,4},{6,7},{7,6},{8,9},{9,8},{10,11... | collective-permute-start | bytes 786440 | tf_op jit(solution)/shard_map/ppermute | solution.py:178
  21.1 12.5 %collective-permute-start.7 = (bf16[2,128,512]{2,1,0:T(8,128)(2,1)S(1)}, bf16[2,128,512]{2,1,0:T(8,128)(2,1)S(1)}, u32[]{:S(2)}, u32[]{:S(2)}) collective-permute-start(bf16[2,128,512]{2,1,0:T(8,128)(2,1)S(1)} %collective-permute-done.6.refs_6_), channel_id=1, source_target_pairs={{0,2},{1,9},{2,4},{3,11},{4,6},{5,13},{6,0},{7,15},{8,10},{9,17},{... | collective-permute-start | bytes 786440 | tf_op jit(solution)/shard_map/ppermute | solution.py:178
  22.2 11.7 %collective-permute-start.8 = (bf16[2,128,512]{2,1,0:T(8,128)(2,1)S(1)}, bf16[2,128,512]{2,1,0:T(8,128)(2,1)}, u32[]{:S(2)}, u32[]{:S(2)}) collective-permute-start(bf16[2,128,512]{2,1,0:T(8,128)(2,1)S(1)} %collective-permute-done.5.refs_3_), channel_id=1, source_target_pairs={{0,6},{1,25},{2,0},{3,27},{4,2},{5,29},{6,4},{7,31},{8,14},{9,1},{... | collective-permute-start | bytes 786440 | tf_op jit(solution)/shard_map/ppermute | solution.py:178
  27.2 15.2 %all-to-all-start = ((bf16[32,40,128]{2,1,0:T(8,128)(2,1)}), bf16[32,40,128]{2,1,0:T(8,128)(2,1)S(1)}, u32[]{:S(2)}, u32[]{:S(2)}) async-start(bf16[32,40,128]{2,1,0:T(8,128)(2,1)} %bitcast.5), calls=%async_computation | async-start | bytes 655360 | tf_op jit(solution)/shard_map/all_to_all | solution.py:215
  32.8 9.6 %collective-permute-start.12 = (bf16[2,128,512]{2,1,0:T(8,128)(2,1)S(1)}, bf16[2,128,512]{2,1,0:T(8,128)(2,1)}, u32[]{:S(2)}, u32[]{:S(2)}) collective-permute-start(bf16[2,128,512]{2,1,0:T(8,128)(2,1)S(1)} %collective-permute-done.4.refs_2_), channel_id=1, source_target_pairs={{0,1},{1,0},{2,3},{3,2},{4,5},{5,4},{6,7},{7,6},{8,9},{9,8},{10,11... | collective-permute-start | bytes 786440 | tf_op jit(solution)/shard_map/ppermute | solution.py:178
  33.1 9.3 %collective-permute-start.13 = (bf16[2,128,512]{2,1,0:T(8,128)(2,1)S(1)}, bf16[2,128,512]{2,1,0:T(8,128)(2,1)}, u32[]{:S(2)}, u32[]{:S(2)}) collective-permute-start(bf16[2,128,512]{2,1,0:T(8,128)(2,1)S(1)} %collective-permute-done.5.refs_3_), channel_id=1, source_target_pairs={{0,1},{1,0},{2,3},{3,2},{4,5},{5,4},{6,7},{7,6},{8,9},{9,8},{10,11... | collective-permute-start | bytes 786440 | tf_op jit(solution)/shard_map/ppermute | solution.py:178
  33.4 9.0 %collective-permute-start.17 = (bf16[2,128,512]{2,1,0:T(8,128)(2,1)S(1)}, bf16[2,128,512]{2,1,0:T(8,128)(2,1)}, u32[]{:S(2)}, u32[]{:S(2)}) collective-permute-start(bf16[2,128,512]{2,1,0:T(8,128)(2,1)S(1)} %collective-permute-done.9.refs_7_), channel_id=1, source_target_pairs={{0,1},{1,0},{2,3},{3,2},{4,5},{5,4},{6,7},{7,6},{8,9},{9,8},{10,11... | collective-permute-start | bytes 786440 | tf_op jit(solution)/shard_map/ppermute | solution.py:178
  33.6 8.8 %collective-permute-start.14 = (bf16[2,128,512]{2,1,0:T(8,128)(2,1)S(1)}, bf16[2,128,512]{2,1,0:T(8,128)(2,1)}, u32[]{:S(2)}, u32[]{:S(2)}) collective-permute-start(bf16[2,128,512]{2,1,0:T(8,128)(2,1)S(1)} %collective-permute-done.7.refs_4_), channel_id=1, source_target_pairs={{0,1},{1,0},{2,3},{3,2},{4,5},{5,4},{6,7},{7,6},{8,9},{9,8},{10,11... | collective-permute-start | bytes 786440 | tf_op jit(solution)/shard_map/ppermute | solution.py:178
  33.9 8.5 %collective-permute-start.15 = (bf16[2,128,512]{2,1,0:T(8,128)(2,1)}, bf16[2,128,512]{2,1,0:T(8,128)(2,1)}, u32[]{:S(2)}, u32[]{:S(2)}) collective-permute-start(bf16[2,128,512]{2,1,0:T(8,128)(2,1)} %collective-permute-done.8.refs_5_), channel_id=1, source_target_pairs={{0,1},{1,0},{2,3},{3,2},{4,5},{5,4},{6,7},{7,6},{8,9},{9,8},{10,11... | collective-permute-start | bytes 786440 | tf_op jit(solution)/shard_map/ppermute | solution.py:178
  45.3 5.3 %collective-permute-start.18 = (bf16[40,1024]{1,0:T(8,128)(2,1)S(1)}, bf16[40,1024]{1,0:T(8,128)(2,1)S(1)}, u32[]{:S(2)}, u32[]{:S(2)}) collective-permute-start(bf16[40,1024]{1,0:T(8,128)(2,1)S(1)} %get-tuple-element.13), channel_id=1, source_target_pairs={{0,32},{1,33},{2,34},{3,35},{4,36},{5,37},{6,38},{7,39},{8,40},{9,... | collective-permute-start | bytes 245768 | tf_op jit(solution)/shard_map/ppermute | solution.py:232
  51.1 0.7 collective-permute-start.19
  53.4 0.7 collective-permute-start.21
  54.6 0.7 collective-permute-start.22
  57.0 19.7 %collective-permute-start.24 = (bf16[40,1024]{1,0:T(8,128)(2,1)S(1)}, bf16[40,1024]{1,0:T(8,128)(2,1)S(1)}, u32[]{:S(2)}, u32[]{:S(2)}) collective-permute-start(bf16[40,1024]{1,0:T(8,128)(2,1)S(1)} %fusion.5), channel_id=1, source_target_pairs={{192,224},{193,225},{194,226},{195,227},{196,228},{197,229},{198,2... | collective-permute-start | bytes 245768 | tf_op jit(solution)/shard_map/ppermute | solution.py:241
  (8 other events, 79.4 us)
where the time goes:
time: 98.3 us; the launch traced here: 97.9 us
  starting transfers between devices  29.6 us (30%)
  waiting for transfers between devices  29.5 us (30%)
  blocking collectives  18 us (18%)
  Pallas kernels  12.2 us (12%)
  local copies, waits for them, and re-layouts  4.72 us (5%)
  matrix products  2.89 us (3%)
    ppermute x18, starting transfers between devices, gather_rows(): pp = lambda value, pairs: lax.ppermute(value, 'row', pairs)  18.7 us
    all_to_all x1, blocking collectives, work(): home = lax.all_to_all(out, 'row', 0, 0, tiled=True)  18 us
    ppermute x6, waiting for transfers between devices, work(): came.append(lax.ppermute(sent, 'front', [(step - 1, step)]))  17.5 us
    all_to_all x1, waiting for transfers between devices, work(): lax.all_to_all(pieces.reshape(ROWS, part, SPAN), 'row', 0, 0, tiled=True)  7.09 us
    all_to_all x1, starting transfers between devices, work(): lax.all_to_all(pieces.reshape(ROWS, part, SPAN), 'row', 0, 0, tiled=True)  5.59 us
    ppermute x18, waiting for transfers between devices, gather_rows(): pp = lambda value, pairs: lax.ppermute(value, 'row', pairs)  4.91 us
    ppermute x6, starting transfers between devices, work(): came.append(lax.ppermute(sent, 'front', [(step - 1, step)]))  4.62 us
    pallas_call x1, Pallas kernels, work(): call(hop_kernel, (shape((CARRIED, WIDTH)), shape((CARRIED, CARRIED))), [V...  4.56 us
  transfers between devices with their start and end apart: 26, of which 5 were waited for; matrix products, arithmetic and copies ran while one was open for 1% of the time, Pallas kernels for 6%

commit v1 on v0

--- a/solution.py
+++ b/solution.py
@@ -26,14 +26,23 @@
     return ((x % SIDE) * SIDE + y % SIDE) * 2 + core
 
 
-def shift(second, step):
+def moves(second, step):
     pairs = []
     for x in range(SIDE):
         for y in range(SIDE):
             for core in range(2):
                 along_x = (core == 0) != second
-                pairs.append((place(x, y, core), place(x + step * along_x, y + step * (not along_x), core)))
+                to_x, to_y = (step(x), y) if along_x else (x, step(y))
+                pairs.append((place(x, y, core), place(to_x, to_y, core)))
     return pairs
+
+
+def near_mate(p):
+    return p ^ 1
+
+
+def far_mate(p):
+    return p + 1 if p % 2 else p - 1
 
 
 SWAP = [(place(x, y, c), place(x, y, 1 - c)) for x in range(SIDE) for y in range(SIDE) for c in range(2)]
@@ -84,11 +93,15 @@
 def slots(row, sibling):
     x, y, core = row // (2 * SIDE), (row // 2) % SIDE, row % 2
     who = 1 - core if sibling else core
+    one, two = jnp.where(who == 0, x, y), jnp.where(who == 0, y, x)
+    near = one + 1 - 2 * (one % 2)
+    far = (one + SIDE - 1 + 2 * (one % 2)) % SIDE
+    beyond = far + 1 - 2 * (far % 2)
     for j in range(SIDE):
-        for k in range(SIDE):
-            dx = jnp.where(who == 0, k, j)
-            dy = jnp.where(who == 0, j, k)
-            yield j, k, (((x + dx) % SIDE) * SIDE + (y + dy) % SIDE) * 2 + who
+        for k, held in enumerate((one, near, far, beyond)):
+            other = (two + j) % SIDE
+            at_x, at_y = jnp.where(who == 0, held, other), jnp.where(who == 0, other, held)
+            yield j, k, (at_x * SIDE + at_y) * 2 + who
 
 
 def base_kernel(row, *refs):
@@ -117,7 +130,13 @@
         sent[:, at] = res.astype(BF)
 
 
-def hop_kernel(offsets, eff, coeffs, turn, hop, gath, fall):
+def unfold(carry):
+    rows = jnp.concatenate([carry[:, j * ROWS : (j + 1) * ROWS] for j in range(EACH)], axis=0)
+    return rows - SPAN * lax.broadcasted_iota(I32, (EACH, ROWS), 1)
+
+
+def hop_kernel(carry, eff, coeffs, turn, hop, gath, fall):
+    offsets = unfold(carry[...])
     lane = lax.broadcasted_iota(I32, (2 * EACH, 2 * SPAN), 1)
     for b in range(0, ROWS, 2):
         where = jnp.concatenate([offsets[:, b : b + 1], offsets[:, b + 1 : b + 2] + SPAN], axis=0)
@@ -144,7 +163,8 @@
             hop[:, (t + h - TAIL) * SPAN : (t + h - TAIL + 1) * SPAN] = fall[h].astype(BF)
 
 
-def table_kernel(offsets, order, spread):
+def table_kernel(carry, order, spread):
+    offsets = unfold(carry[...])
     for r in range(0, CARRIED, 128):
         down = r + lax.broadcasted_iota(I32, (128, CARRIED), 0)
         right = lax.broadcasted_iota(I32, (128, CARRIED), 1)
@@ -176,19 +196,16 @@
 
 def gather_rows(own):
     pp = lambda value, pairs: lax.ppermute(value, "row", pairs)
-    half = own.shape[0] // 2
-    right = pp(own, shift(False, -1))
-    left = pp(own, shift(False, 1))
-    far_a = pp(left[:half], shift(False, 1))
-    far_b = pp(right[half:], shift(False, -1))
-    near = jnp.stack([own, right])
-    near_left = pp(near, shift(True, 1))
-    near_right = pp(near, shift(True, -1))
-    rest = jnp.stack([jnp.concatenate([far_a, far_b]), left])
-    rest_right = pp(rest, shift(True, -1))
-    rest_left = pp(rest, shift(True, 1))
-    near_far = pp(near_left, shift(True, 1))
-    rest_far = pp(rest_right, shift(True, -1))
+    up, down = moves(True, lambda p: p + 1), moves(True, lambda p: p - 1)
+    mate = pp(own, moves(False, near_mate))
+    near = jnp.stack([own, mate])
+    rest = pp(near, moves(False, far_mate))
+    near_left = pp(near, up)
+    near_right = pp(near, down)
+    rest_right = pp(rest, down)
+    rest_left = pp(rest, up)
+    near_far = pp(near_left, up)
+    rest_far = pp(rest_right, down)
     mine = [near, rest, near_right, rest_right, near_far, rest_far, near_left, rest_left]
     theirs = [pp(value, SWAP) for value in mine]
     return mine + theirs
@@ -205,6 +222,7 @@
         mask_kernel,
         shape((SPAN, WIDTH)),
         [SMEM] + [HBM] * 3,
+        limit=60,
         scratch=[
             pltpu.SMEM(block_mask.shape, I32),
             pltpu.SMEM(block_starts.shape, I32),
@@ -215,8 +233,9 @@
     got = lax.all_to_all(pieces.reshape(ROWS, part, SPAN), "row", 0, 0, tiled=True)
     parts = gather_rows(own)
 
-    offsets = carry_map[0].reshape(EACH, ROWS) - SPAN * jnp.arange(ROWS, dtype=I32)
-    order, spread = call(table_kernel, (shape((CARRIED, CARRIED)), shape((CARRIED, 8 * SPAN))), [VMEM])(offsets)
+    order, spread = call(
+        table_kernel, (shape((CARRIED, CARRIED)), shape((CARRIED, 8 * SPAN))), [VMEM]
+    )(carry_map)
 
     eff, base, first, sent = call(
         base_kernel,
@@ -235,13 +254,15 @@
         (shape((CARRIED, WIDTH)), shape((CARRIED, CARRIED))),
         [VMEM] * 3,
         scratch=[pltpu.VMEM((WIDTH // 128, CARRIED, 128), F32), pltpu.VMEM((2, CARRIED, SPAN), F32)],
-    )(offsets, eff, block_coeffs)
+    )(carry_map, eff, block_coeffs)
     for step in range(2, fronts):
         sent = (first + mm(came[-1], hop)).astype(BF)
         came.append(lax.ppermute(sent, "front", [(step - 1, step)]))
 
     none = [jnp.zeros_like(sent)] * (7 - len(came))
-    out = call(last_kernel, shape((ROWS, part, SPAN)), [VMEM] * 13)(*came, *none, base, turn, order, spread, got, eff)
+    out = call(last_kernel, shape((ROWS, part, SPAN)), [VMEM] * 13)(
+        *came, *none, base, turn, order, spread, got, eff
+    )
     home = lax.all_to_all(out, "row", 0, 0, tiled=True)
     return home.reshape(cols, SPAN).T[None]
 

time: 98.3 us -> 100 us (1.017)
  local copies, waits for them, and re-layouts: 4.72 us -> 1.89 us
  starting transfers between devices: 29.6 us -> 32 us
  Pallas kernels: 12.2 us -> 13.4 us
  waiting for transfers between devices: 29.5 us -> 30.5 us
    unnamed x13 -> x6, local copies, waits for them, and re-layouts: 3.73 us -> 0.98 us
    all_to_all x1, starting transfers between devices: 5.59 us -> 8.16 us  [work(): lax.all_to_all(pieces.reshape(ROWS, part, SPAN), 'row', 0, 0, tiled=True)]
    all_to_all x1, waiting for transfers between devices: 7.09 us -> 8.24 us  [work(): lax.all_to_all(pieces.reshape(ROWS, part, SPAN), 'row', 0, 0, tiled=True)]
    ppermute x18 -> x16, starting transfers between devices: 18.7 us -> 18.4 us  [gather_rows(): pp = lambda value, pairs: lax.ppermute(value, 'row', pairs)]
    ppermute x18 -> x16, waiting for transfers between devices: 4.91 us -> 4.87 us  [gather_rows(): pp = lambda value, pairs: lax.ppermute(value, 'row', pairs)]
  transfers between devices with their start and end apart: 26 -> 24, of which waited for: 5 -> 4; matrix products, arithmetic and copies ran while one was open for 1% -> 0% of each run, Pallas kernels for 6% -> 7%
where the time goes in v1:
time: 100 us; the launch traced here: 99.9 us
  starting transfers between devices  32 us (32%)
  waiting for transfers between devices  30.5 us (30%)
  blocking collectives  18 us (18%)
  Pallas kernels  13.4 us (13%)
  matrix products  2.86 us (3%)
  local copies, waits for them, and re-layouts  1.89 us (2%)
    ppermute x16, starting transfers between devices, gather_rows(): pp = lambda value, pairs: lax.ppermute(value, 'row', pairs)  18.4 us
    all_to_all x1, blocking collectives, work(): home = lax.all_to_all(out, 'row', 0, 0, tiled=True)  18 us
    ppermute x6, waiting for transfers between devices, work(): came.append(lax.ppermute(sent, 'front', [(step - 1, step)]))  17.4 us
    all_to_all x1, waiting for transfers between devices, work(): lax.all_to_all(pieces.reshape(ROWS, part, SPAN), 'row', 0, 0, tiled=True)  8.24 us
    all_to_all x1, starting transfers between devices, work(): lax.all_to_all(pieces.reshape(ROWS, part, SPAN), 'row', 0, 0, tiled=True)  8.16 us
    ppermute x16, waiting for transfers between devices, gather_rows(): pp = lambda value, pairs: lax.ppermute(value, 'row', pairs)  4.87 us
    pallas_call x1, Pallas kernels, work(): call(hop_kernel, (shape((CARRIED, WIDTH)), shape((CARRIED, CARRIED))), [V...  4.65 us
    ppermute x6, starting transfers between devices, work(): came.append(lax.ppermute(sent, 'front', [(step - 1, step)]))  4.62 us
  transfers between devices with their start and end apart: 24, of which 4 were waited for; matrix products, arithmetic and copies ran while one was open for 0% of the time, Pallas kernels for 7%

profile of v1, /device:TPU:225, one launch (start us, length us, event | category | flops | bytes accessed | tf_op | source)
XLA Modules:
  0.0 99.9 jit_solution(11328715283870005864)
XLA Ops:
  0.0 1.7 %shard_map.64 = bf16[128,512]{1,0:T(8,128)(2,1)} custom-call(s32[1]{0:T(128)} %bitcast.row, s32[1,1,4]{2,1,0:T(1,128)} %mask.1, s32[1,4]{1,0:T(1,128)} %starts.1, bf16[1,128,512]{2,1,0:T(8,128)(2,1)} %refl.1), custom_call_target="tpu_custom_call" | custom-call | tf_op jit(solution)/shard_map/pallas_call | solution.py:221
  1.7 1.4 %collective-permute-start = (bf16[128,512]{1,0:T(8,128)(2,1)}, bf16[128,512]{1,0:T(8,128)(2,1)S(1)}, u32[]{:S(2)}, u32[]{:S(2)}) collective-permute-start(bf16[128,512]{1,0:T(8,128)(2,1)} %shard_map.64), channel_id=1, source_target_pairs={{0,8},{1,3},{2,10},{3,1},{4,12},{5,7},{6,14},{7,5},{8,0},{9,11},{1... | collective-permute-start | bytes 393224 | tf_op jit(solution)/shard_map/ppermute | solution.py:198
  3.1 3.0 %collective-permute-done = bf16[128,512]{1,0:T(8,128)(2,1)S(1)} collective-permute-done((bf16[128,512]{1,0:T(8,128)(2,1)}, bf16[128,512]{1,0:T(8,128)(2,1)S(1)}, u32[]{:S(2)}, u32[]{:S(2)}) %collective-permute-start) | collective-permute-done | bytes 131104 | tf_op jit(solution)/shard_map/ppermute | solution.py:198
  6.1 0.9 pad_maximum_fusion.refs_0_
  7.1 2.8 %collective-permute-start.1 = (bf16[2,128,512]{2,1,0:T(8,128)(2,1)S(1)}, bf16[2,128,512]{2,1,0:T(8,128)(2,1)S(1)}, u32[]{:S(2)}, u32[]{:S(2)}) collective-permute-start(bf16[2,128,512]{2,1,0:T(8,128)(2,1)S(1)} %pad_maximum_fusion.refs_0_), channel_id=1, source_target_pairs={{0,24},{1,7},{2,26},{3,5},{4,28},{5,3},{6,30},{7,1},{8,16},{9,15},... | collective-permute-start | bytes 786440 | tf_op jit(solution)/shard_map/ppermute | solution.py:198
  9.9 1.2 %collective-permute-start.4 = (bf16[2,128,512]{2,1,0:T(8,128)(2,1)S(1)}, bf16[2,128,512]{2,1,0:T(8,128)(2,1)S(1)}, u32[]{:S(2)}, u32[]{:S(2)}) collective-permute-start(bf16[2,128,512]{2,1,0:T(8,128)(2,1)S(1)} %pad_maximum_fusion.refs_0_), channel_id=1, source_target_pairs={{0,2},{1,9},{2,4},{3,11},{4,6},{5,13},{6,0},{7,15},{8,10},{9,17},{... | collective-permute-start | bytes 786440 | tf_op jit(solution)/shard_map/ppermute | solution.py:198
  11.1 1.5 %collective-permute-start.2 = (bf16[2,128,512]{2,1,0:T(8,128)(2,1)S(1)}, bf16[2,128,512]{2,1,0:T(8,128)(2,1)S(1)}, u32[]{:S(2)}, u32[]{:S(2)}) collective-permute-start(bf16[2,128,512]{2,1,0:T(8,128)(2,1)S(1)} %pad_maximum_fusion.refs_0_), channel_id=1, source_target_pairs={{0,6},{1,25},{2,0},{3,27},{4,2},{5,29},{6,4},{7,31},{8,14},{9,1},{... | collective-permute-start | bytes 786440 | tf_op jit(solution)/shard_map/ppermute | solution.py:198
  12.6 2.1 %collective-permute-start.8 = (bf16[2,128,512]{2,1,0:T(8,128)(2,1)S(1)}, bf16[2,128,512]{2,1,0:T(8,128)(2,1)S(1)}, u32[]{:S(2)}, u32[]{:S(2)}) collective-permute-start(bf16[2,128,512]{2,1,0:T(8,128)(2,1)S(1)} %pad_maximum_fusion.refs_0_), channel_id=1, source_target_pairs={{0,1},{1,0},{2,3},{3,2},{4,5},{5,4},{6,7},{7,6},{8,9},{9,8},{10,11... | collective-permute-start | bytes 786440 | tf_op jit(solution)/shard_map/ppermute | solution.py:198
  14.7 2.1 %collective-permute-start.3 = (bf16[2,128,512]{2,1,0:T(8,128)(2,1)S(1)}, bf16[2,128,512]{2,1,0:T(8,128)(2,1)S(1)}, u32[]{:S(2)}, u32[]{:S(2)}) collective-permute-start(bf16[2,128,512]{2,1,0:T(8,128)(2,1)S(1)} %collective-permute-done.1.refs_1_), channel_id=1, source_target_pairs={{0,6},{1,25},{2,0},{3,27},{4,2},{5,29},{6,4},{7,31},{8,14},{9,1},{... | collective-permute-start | bytes 786440 | tf_op jit(solution)/shard_map/ppermute | solution.py:198
  16.8 1.8 %collective-permute-done.4.refs_6_ = bf16[2,128,512]{2,1,0:T(8,128)(2,1)S(1)} collective-permute-done((bf16[2,128,512]{2,1,0:T(8,128)(2,1)S(1)}, bf16[2,128,512]{2,1,0:T(8,128)(2,1)S(1)}, u32[]{:S(2)}, u32[]{:S(2)}) %collective-permute-start.4) | collective-permute-done | bytes 262176 | tf_op jit(solution)/shard_map/ppermute | solution.py:198
  18.6 1.6 %collective-permute-start.14 = (bf16[2,128,512]{2,1,0:T(8,128)(2,1)S(1)}, bf16[2,128,512]{2,1,0:T(8,128)(2,1)S(1)}, u32[]{:S(2)}, u32[]{:S(2)}) collective-permute-start(bf16[2,128,512]{2,1,0:T(8,128)(2,1)S(1)} %collective-permute-done.4.refs_6_), channel_id=1, source_target_pairs={{0,1},{1,0},{2,3},{3,2},{4,5},{5,4},{6,7},{7,6},{8,9},{9,8},{10,11... | collective-permute-start | bytes 786440 | tf_op jit(solution)/shard_map/ppermute | solution.py:198
  20.2 1.6 %collective-permute-start.5 = (bf16[2,128,512]{2,1,0:T(8,128)(2,1)S(1)}, bf16[2,128,512]{2,1,0:T(8,128)(2,1)S(1)}, u32[]{:S(2)}, u32[]{:S(2)}) collective-permute-start(bf16[2,128,512]{2,1,0:T(8,128)(2,1)S(1)} %collective-permute-done.4.refs_6_), channel_id=1, source_target_pairs={{0,2},{1,9},{2,4},{3,11},{4,6},{5,13},{6,0},{7,15},{8,10},{9,17},{... | collective-permute-start | bytes 786440 | tf_op jit(solution)/shard_map/ppermute | solution.py:198
  21.9 2.7 %collective-permute-start.6 = (bf16[2,128,512]{2,1,0:T(8,128)(2,1)S(1)}, bf16[2,128,512]{2,1,0:T(8,128)(2,1)}, u32[]{:S(2)}, u32[]{:S(2)}) collective-permute-start(bf16[2,128,512]{2,1,0:T(8,128)(2,1)S(1)} %collective-permute-done.3.refs_3_), channel_id=1, source_target_pairs={{0,6},{1,25},{2,0},{3,27},{4,2},{5,29},{6,4},{7,31},{8,14},{9,1},{... | collective-permute-start | bytes 786440 | tf_op jit(solution)/shard_map/ppermute | solution.py:198
  24.6 1.0 copy-done.1
  26.4 8.2 %all-to-all-start = ((bf16[32,40,128]{2,1,0:T(8,128)(2,1)}), bf16[32,40,128]{2,1,0:T(8,128)(2,1)S(1)}, u32[]{:S(2)}, u32[]{:S(2)}) async-start(bf16[32,40,128]{2,1,0:T(8,128)(2,1)} %bitcast.3), calls=%async_computation | async-start | bytes 655360 | tf_op jit(solution)/shard_map/all_to_all | solution.py:233
  35.9 8.2 %all-to-all-done.refs_16_.got = bf16[32,40,128]{2,1,0:T(8,128)(2,1)S(1)} async-done(((bf16[32,40,128]{2,1,0:T(8,128)(2,1)}), bf16[32,40,128]{2,1,0:T(8,128)(2,1)S(1)}, u32[]{:S(2)}, u32[]{:S(2)}) %all-to-all-start) | async-done | bytes 327712 | tf_op jit(solution)/shard_map/all_to_all | solution.py:233
  44.2 2.9 %shard_map.66 = (bf16[32,128,512]{2,1,0:T(8,128)(2,1)S(1)}, f32[40,512]{1,0:T(8,128)S(1)}, f32[40,1024]{1,0:T(8,128)S(1)}, bf16[40,1024]{1,0:T(8,128)(2,1)S(1)}) custom-call(s32[1]{0:T(128)} %bitcast.row, bf16[2,128,512]{2,1,0:T(8,128)(2,1)S(1)} %pad_maximum_fusion.refs_0_, bf16[2,128,512]{2,1,0:T(8,128)(2,1)S(1)} %collective-permute-done.1.refs_1_, ...), custom_call_target="tpu_custom_call" | custom-call | tf_op jit(solution)/shard_map/pallas_call | solution.py:240
  48.0 4.6 %shard_map.67 = (bf16[1024,512]{1,0:T(8,128)(2,1)S(1)}, bf16[1024,1024]{1,0:T(8,128)(2,1)S(1)}) custom-call(s32[1,1024]{1,0:T(1,128)S(1)} %copy-done.2, bf16[32,128,512]{2,1,0:T(8,128)(2,1)S(1)} %get-tuple-element.15.eff, bf16[1,512,512]{2,1,0:T(8,128)(2,1)S(1)} %copy-done), custom_call_target="tpu_custom_call" | custom-call | tf_op jit(solution)/shard_map/pallas_call | solution.py:252
  59.0 1.3 %collective-permute-start.22 = (bf16[40,1024]{1,0:T(8,128)(2,1)S(1)}, bf16[40,1024]{1,0:T(8,128)(2,1)S(1)}, u32[]{:S(2)}, u32[]{:S(2)}) collective-permute-start(bf16[40,1024]{1,0:T(8,128)(2,1)S(1)} %fusion.5), channel_id=1, source_target_pairs={{192,224},{193,225},{194,226},{195,227},{196,228},{197,229},{198,2... | collective-permute-start | bytes 245768 | tf_op jit(solution)/shard_map/ppermute | solution.py:260
  60.3 1.0 %shard_map.68 = (bf16[1024,1024]{1,0:T(8,128)(2,1)S(1)}, bf16[1024,1024]{1,0:T(8,128)(2,1)S(1)}) custom-call(s32[1,1024]{1,0:T(1,128)S(1)} %copy-done.2), custom_call_target="tpu_custom_call" | custom-call | tf_op jit(solution)/shard_map/pallas_call | solution.py:236
  61.3 17.4 %collective-permute-done.22.c7 = bf16[40,1024]{1,0:T(8,128)(2,1)S(1)} collective-permute-done((bf16[40,1024]{1,0:T(8,128)(2,1)S(1)}, bf16[40,1024]{1,0:T(8,128)(2,1)S(1)}, u32[]{:S(2)}, u32[]{:S(2)}) %collective-permute-start.22) | collective-permute-done | bytes 81952 | tf_op jit(solution)/shard_map/ppermute | solution.py:260
  78.7 2.2 %shard_map.69 = bf16[32,40,128]{2,1,0:T(8,128)(2,1)S(1)} custom-call(bf16[40,1024]{1,0:T(8,128)(2,1)S(1)} %collective-permute-done.16.c1, bf16[40,1024]{1,0:T(8,128)(2,1)S(1)} %collective-permute-done.17.c2, bf16[40,1024]{1,0:T(8,128)(2,1)S(1)} %collective-permute-done.18.c3, bf16[40,1024]{1,0:T(8,128)(2,1)S(1)} %collective-permute-done.19.c4, ...), custom_call_target="tpu_custom_call" | custom-call | tf_op jit(solution)/shard_map/pallas_call | solution.py:263
  80.9 18.0 %all_to_all.10 = bf16[32,40,128]{2,1,0:T(8,128)(2,1)S(1)} all-to-all(bf16[32,40,128]{2,1,0:T(8,128)(2,1)S(1)} %shard_map.69), channel_id=1, replica_groups=mesh['front'=8,'row'=32] {'row'}, dimensions={0} | all-to-all | bytes 655360 | tf_op jit(solution)/shard_map/all_to_all | solution.py:266
  99.0 0.9 copy.7
  (45 shorter events, 9.4 us)
Async XLA Ops:
  1.7 4.4 %collective-permute-start = (bf16[128,512]{1,0:T(8,128)(2,1)}, bf16[128,512]{1,0:T(8,128)(2,1)S(1)}, u32[]{:S(2)}, u32[]{:S(2)}) collective-permute-start(bf16[128,512]{1,0:T(8,128)(2,1)} %shard_map.64), channel_id=1, source_target_pairs={{0,8},{1,3},{2,10},{3,1},{4,12},{5,7},{6,14},{7,5},{8,0},{9,11},{1... | collective-permute-start | bytes 393224 | tf_op jit(solution)/shard_map/ppermute | solution.py:198
  7.1 7.6 %collective-permute-start.1 = (bf16[2,128,512]{2,1,0:T(8,128)(2,1)S(1)}, bf16[2,128,512]{2,1,0:T(8,128)(2,1)S(1)}, u32[]{:S(2)}, u32[]{:S(2)}) collective-permute-start(bf16[2,128,512]{2,1,0:T(8,128)(2,1)S(1)} %pad_maximum_fusion.refs_0_), channel_id=1, source_target_pairs={{0,24},{1,7},{2,26},{3,5},{4,28},{5,3},{6,30},{7,1},{8,16},{9,15},... | collective-permute-start | bytes 786440 | tf_op jit(solution)/shard_map/ppermute | solution.py:198
  9.9 8.7 %collective-permute-start.4 = (bf16[2,128,512]{2,1,0:T(8,128)(2,1)S(1)}, bf16[2,128,512]{2,1,0:T(8,128)(2,1)S(1)}, u32[]{:S(2)}, u32[]{:S(2)}) collective-permute-start(bf16[2,128,512]{2,1,0:T(8,128)(2,1)S(1)} %pad_maximum_fusion.refs_0_), channel_id=1, source_target_pairs={{0,2},{1,9},{2,4},{3,11},{4,6},{5,13},{6,0},{7,15},{8,10},{9,17},{... | collective-permute-start | bytes 786440 | tf_op jit(solution)/shard_map/ppermute | solution.py:198
  11.1 10.7 %collective-permute-start.2 = (bf16[2,128,512]{2,1,0:T(8,128)(2,1)S(1)}, bf16[2,128,512]{2,1,0:T(8,128)(2,1)S(1)}, u32[]{:S(2)}, u32[]{:S(2)}) collective-permute-start(bf16[2,128,512]{2,1,0:T(8,128)(2,1)S(1)} %pad_maximum_fusion.refs_0_), channel_id=1, source_target_pairs={{0,6},{1,25},{2,0},{3,27},{4,2},{5,29},{6,4},{7,31},{8,14},{9,1},{... | collective-permute-start | bytes 786440 | tf_op jit(solution)/shard_map/ppermute | solution.py:198
  12.6 9.2 %collective-permute-start.8 = (bf16[2,128,512]{2,1,0:T(8,128)(2,1)S(1)}, bf16[2,128,512]{2,1,0:T(8,128)(2,1)S(1)}, u32[]{:S(2)}, u32[]{:S(2)}) collective-permute-start(bf16[2,128,512]{2,1,0:T(8,128)(2,1)S(1)} %pad_maximum_fusion.refs_0_), channel_id=1, source_target_pairs={{0,1},{1,0},{2,3},{3,2},{4,5},{5,4},{6,7},{7,6},{8,9},{9,8},{10,11... | collective-permute-start | bytes 786440 | tf_op jit(solution)/shard_map/ppermute | solution.py:198
  14.7 7.2 %collective-permute-start.3 = (bf16[2,128,512]{2,1,0:T(8,128)(2,1)S(1)}, bf16[2,128,512]{2,1,0:T(8,128)(2,1)S(1)}, u32[]{:S(2)}, u32[]{:S(2)}) collective-permute-start(bf16[2,128,512]{2,1,0:T(8,128)(2,1)S(1)} %collective-permute-done.1.refs_1_), channel_id=1, source_target_pairs={{0,6},{1,25},{2,0},{3,27},{4,2},{5,29},{6,4},{7,31},{8,14},{9,1},{... | collective-permute-start | bytes 786440 | tf_op jit(solution)/shard_map/ppermute | solution.py:198
  18.6 15.9 %collective-permute-start.14 = (bf16[2,128,512]{2,1,0:T(8,128)(2,1)S(1)}, bf16[2,128,512]{2,1,0:T(8,128)(2,1)S(1)}, u32[]{:S(2)}, u32[]{:S(2)}) collective-permute-start(bf16[2,128,512]{2,1,0:T(8,128)(2,1)S(1)} %collective-permute-done.4.refs_6_), channel_id=1, source_target_pairs={{0,1},{1,0},{2,3},{3,2},{4,5},{5,4},{6,7},{7,6},{8,9},{9,8},{10,11... | collective-permute-start | bytes 786440 | tf_op jit(solution)/shard_map/ppermute | solution.py:198
  20.2 14.7 %collective-permute-start.5 = (bf16[2,128,512]{2,1,0:T(8,128)(2,1)S(1)}, bf16[2,128,512]{2,1,0:T(8,128)(2,1)S(1)}, u32[]{:S(2)}, u32[]{:S(2)}) collective-permute-start(bf16[2,128,512]{2,1,0:T(8,128)(2,1)S(1)} %collective-permute-done.4.refs_6_), channel_id=1, source_target_pairs={{0,2},{1,9},{2,4},{3,11},{4,6},{5,13},{6,0},{7,15},{8,10},{9,17},{... | collective-permute-start | bytes 786440 | tf_op jit(solution)/shard_map/ppermute | solution.py:198
  21.8 13.4 %collective-permute-start.10 = (bf16[2,128,512]{2,1,0:T(8,128)(2,1)S(1)}, bf16[2,128,512]{2,1,0:T(8,128)(2,1)S(1)}, u32[]{:S(2)}, u32[]{:S(2)}) collective-permute-start(bf16[2,128,512]{2,1,0:T(8,128)(2,1)S(1)} %collective-permute-done.2.refs_2_), channel_id=1, source_target_pairs={{0,1},{1,0},{2,3},{3,2},{4,5},{5,4},{6,7},{7,6},{8,9},{9,8},{10,11... | collective-permute-start | bytes 786440 | tf_op jit(solution)/shard_map/ppermute | solution.py:198
  21.8 13.6 %collective-permute-start.7 = (bf16[2,128,512]{2,1,0:T(8,128)(2,1)S(1)}, bf16[2,128,512]{2,1,0:T(8,128)(2,1)S(1)}, u32[]{:S(2)}, u32[]{:S(2)}) collective-permute-start(bf16[2,128,512]{2,1,0:T(8,128)(2,1)S(1)} %collective-permute-done.1.refs_1_), channel_id=1, source_target_pairs={{0,2},{1,9},{2,4},{3,11},{4,6},{5,13},{6,0},{7,15},{8,10},{9,17},{... | collective-permute-start | bytes 786440 | tf_op jit(solution)/shard_map/ppermute | solution.py:198
  21.9 13.8 %collective-permute-start.6 = (bf16[2,128,512]{2,1,0:T(8,128)(2,1)S(1)}, bf16[2,128,512]{2,1,0:T(8,128)(2,1)}, u32[]{:S(2)}, u32[]{:S(2)}) collective-permute-start(bf16[2,128,512]{2,1,0:T(8,128)(2,1)S(1)} %collective-permute-done.3.refs_3_), channel_id=1, source_target_pairs={{0,6},{1,25},{2,0},{3,27},{4,2},{5,29},{6,4},{7,31},{8,14},{9,1},{... | collective-permute-start | bytes 786440 | tf_op jit(solution)/shard_map/ppermute | solution.py:198
  26.4 17.8 %all-to-all-start = ((bf16[32,40,128]{2,1,0:T(8,128)(2,1)}), bf16[32,40,128]{2,1,0:T(8,128)(2,1)S(1)}, u32[]{:S(2)}, u32[]{:S(2)}) async-start(bf16[32,40,128]{2,1,0:T(8,128)(2,1)} %bitcast.3), calls=%async_computation | async-start | bytes 655360 | tf_op jit(solution)/shard_map/all_to_all | solution.py:233
  34.6 9.6 %collective-permute-start.9 = (bf16[2,128,512]{2,1,0:T(8,128)(2,1)S(1)}, bf16[2,128,512]{2,1,0:T(8,128)(2,1)}, u32[]{:S(2)}, u32[]{:S(2)}) collective-permute-start(bf16[2,128,512]{2,1,0:T(8,128)(2,1)S(1)} %collective-permute-done.1.refs_1_), channel_id=1, source_target_pairs={{0,1},{1,0},{2,3},{3,2},{4,5},{5,4},{6,7},{7,6},{8,9},{9,8},{10,11... | collective-permute-start | bytes 786440 | tf_op jit(solution)/shard_map/ppermute | solution.py:198
  34.9 9.3 %collective-permute-start.11 = (bf16[2,128,512]{2,1,0:T(8,128)(2,1)S(1)}, bf16[2,128,512]{2,1,0:T(8,128)(2,1)}, u32[]{:S(2)}, u32[]{:S(2)}) collective-permute-start(bf16[2,128,512]{2,1,0:T(8,128)(2,1)S(1)} %collective-permute-done.3.refs_3_), channel_id=1, source_target_pairs={{0,1},{1,0},{2,3},{3,2},{4,5},{5,4},{6,7},{7,6},{8,9},{9,8},{10,11... | collective-permute-start | bytes 786440 | tf_op jit(solution)/shard_map/ppermute | solution.py:198
  35.2 9.0 %collective-permute-start.12 = (bf16[2,128,512]{2,1,0:T(8,128)(2,1)S(1)}, bf16[2,128,512]{2,1,0:T(8,128)(2,1)}, u32[]{:S(2)}, u32[]{:S(2)}) collective-permute-start(bf16[2,128,512]{2,1,0:T(8,128)(2,1)S(1)} %collective-permute-done.5.refs_4_), channel_id=1, source_target_pairs={{0,1},{1,0},{2,3},{3,2},{4,5},{5,4},{6,7},{7,6},{8,9},{9,8},{10,11... | collective-permute-start | bytes 786440 | tf_op jit(solution)/shard_map/ppermute | solution.py:198
  35.4 8.8 %collective-permute-start.15 = (bf16[2,128,512]{2,1,0:T(8,128)(2,1)S(1)}, bf16[2,128,512]{2,1,0:T(8,128)(2,1)}, u32[]{:S(2)}, u32[]{:S(2)}) collective-permute-start(bf16[2,128,512]{2,1,0:T(8,128)(2,1)S(1)} %collective-permute-done.7.refs_7_), channel_id=1, source_target_pairs={{0,1},{1,0},{2,3},{3,2},{4,5},{5,4},{6,7},{7,6},{8,9},{9,8},{10,11... | collective-permute-start | bytes 786440 | tf_op jit(solution)/shard_map/ppermute | solution.py:198
  35.7 8.5 %collective-permute-start.13 = (bf16[2,128,512]{2,1,0:T(8,128)(2,1)}, bf16[2,128,512]{2,1,0:T(8,128)(2,1)}, u32[]{:S(2)}, u32[]{:S(2)}) collective-permute-start(bf16[2,128,512]{2,1,0:T(8,128)(2,1)} %collective-permute-done.6.refs_5_), channel_id=1, source_target_pairs={{0,1},{1,0},{2,3},{3,2},{4,5},{5,4},{6,7},{7,6},{8,9},{9,8},{10,11... | collective-permute-start | bytes 786440 | tf_op jit(solution)/shard_map/ppermute | solution.py:198
  47.1 5.5 %collective-permute-start.16 = (bf16[40,1024]{1,0:T(8,128)(2,1)S(1)}, bf16[40,1024]{1,0:T(8,128)(2,1)S(1)}, u32[]{:S(2)}, u32[]{:S(2)}) collective-permute-start(bf16[40,1024]{1,0:T(8,128)(2,1)S(1)} %get-tuple-element.13), channel_id=1, source_target_pairs={{0,32},{1,33},{2,34},{3,35},{4,36},{5,37},{6,38},{7,39},{8,40},{9,... | collective-permute-start | bytes 245768 | tf_op jit(solution)/shard_map/ppermute | solution.py:251
  53.1 0.7 collective-permute-start.17
  54.3 0.7 collective-permute-start.18
  55.5 0.7 collective-permute-start.19
  56.6 0.7 collective-permute-start.20
  57.8 0.7 collective-permute-start.21
  59.0 19.7 %collective-permute-start.22 = (bf16[40,1024]{1,0:T(8,128)(2,1)S(1)}, bf16[40,1024]{1,0:T(8,128)(2,1)S(1)}, u32[]{:S(2)}, u32[]{:S(2)}) collective-permute-start(bf16[40,1024]{1,0:T(8,128)(2,1)S(1)} %fusion.5), channel_id=1, source_target_pairs={{192,224},{193,225},{194,226},{195,227},{196,228},{197,229},{198,2... | collective-permute-start | bytes 245768 | tf_op jit(solution)/shard_map/ppermute | solution.py:260
  (3 other events, 58.6 us)

commit v2 on v1

--- a/solution.py
+++ b/solution.py
@@ -14,6 +14,7 @@
 SPAN = 128
 EACH = 32
 CARRIED = ROWS * EACH
+QUARTER = CARRIED // 4
 TAIL = 24
 WIDTH = 512
 
@@ -48,11 +49,10 @@
 SWAP = [(place(x, y, c), place(x, y, 1 - c)) for x in range(SIDE) for y in range(SIDE) for c in range(2)]
 
 VMEM = pl.BlockSpec(memory_space=pltpu.VMEM)
-SMEM = pl.BlockSpec(memory_space=pltpu.SMEM)
 HBM = pl.BlockSpec(memory_space=pltpu.HBM)
 
 
-def call(kernel, outs, specs, limit=20, scratch=(), cost=None):
+def call(kernel, outs, specs, limit=8, scratch=()):
     return pl.pallas_call(
         kernel,
         out_shape=outs,
@@ -60,7 +60,6 @@
         out_specs=jax.tree.map(lambda _: VMEM, outs),
         scratch_shapes=scratch,
         compiler_params=pltpu.CompilerParams(vmem_limit_bytes=limit << 20),
-        cost_estimate=cost,
     )
 
 
@@ -68,16 +67,16 @@
     return jax.ShapeDtypeStruct(dims, dtype)
 
 
-def mask_kernel(row, mask, starts, refl, own, mask_s, starts_s, refl_v, sems):
-    moves = [
+def mask_kernel(mask, starts, refl, own, mask_s, starts_s, refl_v, sems):
+    fetches = [
         pltpu.make_async_copy(source, target, sems.at[i])
         for i, (source, target) in enumerate(((refl, refl_v), (mask, mask_s), (starts, starts_s)))
     ]
-    for move in moves:
-        move.start()
-    for move in moves:
-        move.wait()
-    ids = row[0] * SPAN + lax.broadcasted_iota(I32, (SPAN, 128), 0)
+    for fetch in fetches:
+        fetch.start()
+    for fetch in fetches:
+        fetch.wait()
+    ids = lax.axis_index("row") * SPAN + lax.broadcasted_iota(I32, (SPAN, 128), 0)
     for k in range(WIDTH // 128):
         kept = (ids >= starts_s[0, k]) & (mask_s[0, 0, k] == 1)
         part = refl_v[0, :, k * 128 : (k + 1) * 128].astype(F32)
@@ -104,38 +103,60 @@
             yield j, k, (at_x * SIDE + at_y) * 2 + who
 
 
-def base_kernel(row, *refs):
-    mine, theirs, (got, coeffs, eff, base, first, sent) = refs[:8], refs[8:16], refs[16:]
-    acc = jnp.zeros(base.shape, F32)
+def product(row, mine, theirs, got, eff, acc):
     for sibling, parts in enumerate((mine, theirs)):
         held = None
-        for j, k, block in slots(row[0], sibling):
+        for j, k, block in slots(row, sibling):
             tile = parts[2 * j + k // 2][k % 2]
-            eff[block] = tile
+            if eff is not None:
+                eff[block] = tile
             if held is None:
                 held = (got[block], tile)
             else:
                 lhs = jnp.concatenate([held[0], got[block]], axis=1)
                 acc += mm(lhs, jnp.concatenate([held[1], tile], axis=0))
                 held = None
+    return acc
+
+
+def first_kernel(*refs):
+    mine, theirs, (got, coeffs, sent) = refs[:8], refs[8:16], refs[16:]
+
+    front = lax.axis_index("front")
+
+    @pl.when(front != 0)
+    def _():
+        sent[...] = jnp.zeros_like(sent)
+
+    @pl.when(front == 0)
+    def _():
+        row = lax.axis_index("row")
+        acc = product(row, mine, theirs, got, None, jnp.zeros((sent.shape[0], WIDTH), F32))
+        m = mm(acc.astype(BF), coeffs[0]).astype(BF)
+        for sibling, parts in enumerate((mine, theirs)):
+            for j, k, block in slots(row, sibling):
+
+                @pl.when(block >= TAIL)
+                def _():
+                    res = got[block].astype(F32) - mm(m, parts[2 * j + k // 2][k % 2], ((1,), (1,)))
+                    sent[:, pl.ds(pl.multiple_of((block - TAIL) * SPAN, SPAN), SPAN)] = res.astype(BF)
+
+
+def unfold(carry):
+    rows = jnp.concatenate([carry[:, j * ROWS : (j + 1) * ROWS] for j in range(EACH)], axis=0)
+    return rows - SPAN * lax.broadcasted_iota(I32, (EACH, ROWS), 1)
+
+
+def base_kernel(*refs):
+    mine, theirs, (got, coeffs, carry, eff, base, first, gath, wide) = refs[:8], refs[8:16], refs[16:]
+    acc = product(lax.axis_index("row"), mine, theirs, got, eff, jnp.zeros(base.shape, F32))
     m = mm(acc.astype(BF), coeffs[0])
     base[...] = m
     m = m.astype(BF)
     for t in range(TAIL, ROWS, 2):
         low = eff[t : t + 2].reshape(2 * SPAN, WIDTH)
         have = jnp.concatenate([got[t], got[t + 1]], axis=1).astype(F32)
-        res = have - mm(m, low, ((1,), (1,)))
-        at = pl.ds((t - TAIL) * SPAN, 2 * SPAN)
-        first[:, at] = res
-        sent[:, at] = res.astype(BF)
-
-
-def unfold(carry):
-    rows = jnp.concatenate([carry[:, j * ROWS : (j + 1) * ROWS] for j in range(EACH)], axis=0)
-    return rows - SPAN * lax.broadcasted_iota(I32, (EACH, ROWS), 1)
-
-
-def hop_kernel(carry, eff, coeffs, turn, hop, gath, fall):
+        first[:, (t - TAIL) * SPAN : (t - TAIL + 2) * SPAN] = have - mm(m, low, ((1,), (1,)))
     offsets = unfold(carry[...])
     lane = lax.broadcasted_iota(I32, (2 * EACH, 2 * SPAN), 1)
     for b in range(0, ROWS, 2):
@@ -145,10 +166,27 @@
         for h in range(2):
             for k in range(WIDTH // 128):
                 tile = rows[h * EACH : (h + 1) * EACH, k * 128 : (k + 1) * 128]
-                gath[k, pl.ds(b + h, EACH, stride=ROWS), :] = tile
+                wide[k, pl.ds(b + h, EACH, stride=ROWS), :] = tile
+    for k in range(WIDTH // 128):
+        gath[:, k * 128 : (k + 1) * 128] = wide[k].astype(BF)
+
+
+def second_kernel(came, first, gath, coeffs, eff, order, spread, sent):
+    cin = came[...]
+    w = mm(cin, gath[...]).astype(BF)
+    t = mm(w, coeffs[0]).astype(BF)
+    placed = mm(cin, order[:, CARRIED - QUARTER :]).astype(BF)
+    moved = mm(placed, spread[CARRIED - QUARTER :, :])
+    for b in range(TAIL, ROWS, 2):
+        at = slice((b - TAIL) * SPAN, (b - TAIL + 2) * SPAN)
+        down = mm(t, eff[b : b + 2].reshape(2 * SPAN, WIDTH), ((1,), (1,)))
+        sent[:, at] = (first[:, at] + moved[:, at] - down).astype(BF)
+
+
+def hop_kernel(carry, gath, eff, coeffs, turn, hop, fall):
+    offsets = unfold(carry[...])
     for r in range(0, CARRIED, 256):
-        wide = jnp.concatenate([gath[k, r : r + 256, :].astype(BF) for k in range(WIDTH // 128)], axis=1)
-        turn[r : r + 256, :] = mm(wide, coeffs[0]).astype(BF)
+        turn[r : r + 256, :] = mm(gath[r : r + 256, :], coeffs[0]).astype(BF)
     lane = lax.broadcasted_iota(I32, (EACH, SPAN), 1)
     for t in range(TAIL, ROWS, 2):
         low = eff[t : t + 2].reshape(2 * SPAN, WIDTH)
@@ -213,7 +251,6 @@
 
 def work(panels, reflectors, block_coeffs, block_mask, block_starts, carry_map):
     fronts = lax.axis_size("front")
-    row = lax.axis_index("row").reshape(1)
     cols = panels.shape[2]
     part = cols // ROWS
 
@@ -221,7 +258,7 @@
     own = call(
         mask_kernel,
         shape((SPAN, WIDTH)),
-        [SMEM] + [HBM] * 3,
+        [HBM] * 3,
         limit=60,
         scratch=[
             pltpu.SMEM(block_mask.shape, I32),
@@ -229,39 +266,42 @@
             pltpu.VMEM(reflectors.shape, BF),
             pltpu.SemaphoreType.DMA((3,)),
         ],
-    )(row, block_mask, block_starts, reflectors)
+    )(block_mask, block_starts, reflectors)
     got = lax.all_to_all(pieces.reshape(ROWS, part, SPAN), "row", 0, 0, tiled=True)
     parts = gather_rows(own)
-
     order, spread = call(
         table_kernel, (shape((CARRIED, CARRIED)), shape((CARRIED, 8 * SPAN))), [VMEM]
     )(carry_map)
 
-    eff, base, first, sent = call(
+    sent = call(first_kernel, shape((part, CARRIED)), [VMEM] * 18)(*parts, got, block_coeffs)
+    came = [lax.ppermute(sent, "front", [(0, 1)])]
+    eff, base, first, gath = call(
         base_kernel,
         (
             shape((ROWS, SPAN, WIDTH)),
             shape((part, WIDTH), F32),
             shape((part, CARRIED), F32),
-            shape((part, CARRIED)),
+            shape((CARRIED, WIDTH)),
         ),
-        [SMEM] + [VMEM] * 18,
-    )(row, *parts, got, block_coeffs)
-
-    came = [lax.ppermute(sent, "front", [(0, 1)])]
+        [VMEM] * 19,
+        scratch=[pltpu.VMEM((WIDTH // 128, CARRIED, 128), F32)],
+    )(*parts, got, block_coeffs, carry_map)
+    sent = call(second_kernel, shape((part, CARRIED)), [VMEM] * 7)(
+        came[0], first, gath, block_coeffs, eff, order, spread
+    )
+    came.append(lax.ppermute(sent, "front", [(1, 2)]))
     turn, hop = call(
         hop_kernel,
         (shape((CARRIED, WIDTH)), shape((CARRIED, CARRIED))),
-        [VMEM] * 3,
-        scratch=[pltpu.VMEM((WIDTH // 128, CARRIED, 128), F32), pltpu.VMEM((2, CARRIED, SPAN), F32)],
-    )(carry_map, eff, block_coeffs)
-    for step in range(2, fronts):
+        [VMEM] * 4,
+        scratch=[pltpu.VMEM((2, CARRIED, SPAN), F32)],
+    )(carry_map, gath, eff, block_coeffs)
+    for step in range(3, fronts):
         sent = (first + mm(came[-1], hop)).astype(BF)
         came.append(lax.ppermute(sent, "front", [(step - 1, step)]))
 
-    none = [jnp.zeros_like(sent)] * (7 - len(came))
     out = call(last_kernel, shape((ROWS, part, SPAN)), [VMEM] * 13)(
-        *came, *none, base, turn, order, spread, got, eff
+        *came, *[jnp.zeros_like(sent)] * (7 - len(came)), base, turn, order, spread, got, eff
     )
     home = lax.all_to_all(out, "row", 0, 0, tiled=True)
     return home.reshape(cols, SPAN).T[None]

time: 100 us -> 101 us (1.010)
  Pallas kernels: 13.4 us -> 16 us
  waiting for transfers between devices: 30.5 us -> 29.4 us
    pallas_call x1, Pallas kernels: 2.89 us -> 5.49 us  [work(): call(base_kernel, (shape((ROWS, SPAN, WIDTH)), shape((part, WIDTH), F32),...]
    pallas_call x1, Pallas kernels: 4.65 us -> 2.15 us  [work(): call(hop_kernel, (shape((CARRIED, WIDTH)), shape((CARRIED, CARRIED))), [V...]
    pallas_call x1 -> x3, Pallas kernels: 1.71 us -> 4.17 us  [the longest x1 1.71 us: work(): call(mask_kernel, shape((SPAN, WIDTH)), [HBM] * 3, limit=60, scratch=[plt...]
    ppermute x6 -> x5, waiting for transfers between devices: 17.4 us -> 16.3 us  [work(): came.append(lax.ppermute(sent, 'front', [(step - 1, step)]))]
    ppermute x6 -> x5, starting transfers between devices: 4.62 us -> 3.96 us  [work(): came.append(lax.ppermute(sent, 'front', [(step - 1, step)]))]
    dot_general x6 -> x5, matrix products: 2.86 us -> 2.41 us  [mm(): return lax.dot_general(a, b, (dims, ((), ())), preferred_element_type=F32)]
  transfers between devices with their start and end apart: 24 -> 24, of which waited for: 4 -> 4; matrix products, arithmetic and copies ran while one was open for 0% -> 0% of each run, Pallas kernels for 7% -> 9%
where the time goes in v2:
time: 101 us
  starting transfers between devices  31.8 us (31%)
  waiting for transfers between devices  29.4 us (29%)
  blocking collectives  18 us (18%)
  Pallas kernels  16 us (16%)
  matrix products  2.41 us (2%)
  local copies, waits for them, and re-layouts  1.89 us (2%)
    ppermute x16, starting transfers between devices, gather_rows(): pp = lambda value, pairs: lax.ppermute(value, 'row', pairs)  18.4 us
    all_to_all x1, blocking collectives, work(): home = lax.all_to_all(out, 'row', 0, 0, tiled=True)  18 us
    ppermute x5, waiting for transfers between devices, work(): came.append(lax.ppermute(sent, 'front', [(step - 1, step)]))  16.3 us
    all_to_all x1, waiting for transfers between devices, work(): lax.all_to_all(pieces.reshape(ROWS, part, SPAN), 'row', 0, 0, tiled=True)  8.24 us
    all_to_all x1, starting transfers between devices, work(): lax.all_to_all(pieces.reshape(ROWS, part, SPAN), 'row', 0, 0, tiled=True)  8.16 us
    pallas_call x1, Pallas kernels, work(): call(base_kernel, (shape((ROWS, SPAN, WIDTH)), shape((part, WIDTH), F32),...  5.49 us
    ppermute x16, waiting for transfers between devices, gather_rows(): pp = lambda value, pairs: lax.ppermute(value, 'row', pairs)  4.87 us
    ppermute x5, starting transfers between devices, work(): came.append(lax.ppermute(sent, 'front', [(step - 1, step)]))  3.96 us
  transfers between devices with their start and end apart: 24, of which 4 were waited for; matrix products, arithmetic and copies ran while one was open for 0% of the time, Pallas kernels for 9%

profile of v2, /device:TPU:225, one launch (start us, length us, event | category | flops | bytes accessed | tf_op | source)
XLA Modules:
  0.0 100.7 jit_solution(16322920752448533806)
XLA Ops:
  0.0 1.7 %shard_map.64 = bf16[128,512]{1,0:T(8,128)(2,1)} custom-call(s32[1,1,4]{2,1,0:T(1,128)} %mask.1, s32[1,4]{1,0:T(1,128)} %starts.1, bf16[1,128,512]{2,1,0:T(8,128)(2,1)} %refl.1), custom_call_target="tpu_custom_call" | custom-call | tf_op jit(solution)/shard_map/pallas_call | solution.py:258
  1.7 1.4 %collective-permute-start = (bf16[128,512]{1,0:T(8,128)(2,1)}, bf16[128,512]{1,0:T(8,128)(2,1)S(1)}, u32[]{:S(2)}, u32[]{:S(2)}) collective-permute-start(bf16[128,512]{1,0:T(8,128)(2,1)} %shard_map.64), channel_id=1, source_target_pairs={{0,8},{1,3},{2,10},{3,1},{4,12},{5,7},{6,14},{7,5},{8,0},{9,11},{1... | collective-permute-start | bytes 393224 | tf_op jit(solution)/shard_map/ppermute | solution.py:236
  3.1 3.0 %collective-permute-done = bf16[128,512]{1,0:T(8,128)(2,1)S(1)} collective-permute-done((bf16[128,512]{1,0:T(8,128)(2,1)}, bf16[128,512]{1,0:T(8,128)(2,1)S(1)}, u32[]{:S(2)}, u32[]{:S(2)}) %collective-permute-start) | collective-permute-done | bytes 131104 | tf_op jit(solution)/shard_map/ppermute | solution.py:236
  7.1 2.8 %collective-permute-start.1 = (bf16[2,128,512]{2,1,0:T(8,128)(2,1)S(1)}, bf16[2,128,512]{2,1,0:T(8,128)(2,1)S(1)}, u32[]{:S(2)}, u32[]{:S(2)}) collective-permute-start(bf16[2,128,512]{2,1,0:T(8,128)(2,1)S(1)} %pad_maximum_fusion.refs_0_), channel_id=1, source_target_pairs={{0,24},{1,7},{2,26},{3,5},{4,28},{5,3},{6,30},{7,1},{8,16},{9,15},... | collective-permute-start | bytes 786440 | tf_op jit(solution)/shard_map/ppermute | solution.py:236
  9.9 1.2 %collective-permute-start.4 = (bf16[2,128,512]{2,1,0:T(8,128)(2,1)S(1)}, bf16[2,128,512]{2,1,0:T(8,128)(2,1)S(1)}, u32[]{:S(2)}, u32[]{:S(2)}) collective-permute-start(bf16[2,128,512]{2,1,0:T(8,128)(2,1)S(1)} %pad_maximum_fusion.refs_0_), channel_id=1, source_target_pairs={{0,2},{1,9},{2,4},{3,11},{4,6},{5,13},{6,0},{7,15},{8,10},{9,17},{... | collective-permute-start | bytes 786440 | tf_op jit(solution)/shard_map/ppermute | solution.py:236
  11.1 1.5 %collective-permute-start.2 = (bf16[2,128,512]{2,1,0:T(8,128)(2,1)S(1)}, bf16[2,128,512]{2,1,0:T(8,128)(2,1)S(1)}, u32[]{:S(2)}, u32[]{:S(2)}) collective-permute-start(bf16[2,128,512]{2,1,0:T(8,128)(2,1)S(1)} %pad_maximum_fusion.refs_0_), channel_id=1, source_target_pairs={{0,6},{1,25},{2,0},{3,27},{4,2},{5,29},{6,4},{7,31},{8,14},{9,1},{... | collective-permute-start | bytes 786440 | tf_op jit(solution)/shard_map/ppermute | solution.py:236
  12.6 2.1 %collective-permute-start.8 = (bf16[2,128,512]{2,1,0:T(8,128)(2,1)S(1)}, bf16[2,128,512]{2,1,0:T(8,128)(2,1)S(1)}, u32[]{:S(2)}, u32[]{:S(2)}) collective-permute-start(bf16[2,128,512]{2,1,0:T(8,128)(2,1)S(1)} %pad_maximum_fusion.refs_0_), channel_id=1, source_target_pairs={{0,1},{1,0},{2,3},{3,2},{4,5},{5,4},{6,7},{7,6},{8,9},{9,8},{10,11... | collective-permute-start | bytes 786440 | tf_op jit(solution)/shard_map/ppermute | solution.py:236
  14.7 2.1 %collective-permute-start.3 = (bf16[2,128,512]{2,1,0:T(8,128)(2,1)S(1)}, bf16[2,128,512]{2,1,0:T(8,128)(2,1)S(1)}, u32[]{:S(2)}, u32[]{:S(2)}) collective-permute-start(bf16[2,128,512]{2,1,0:T(8,128)(2,1)S(1)} %collective-permute-done.1.refs_1_), channel_id=1, source_target_pairs={{0,6},{1,25},{2,0},{3,27},{4,2},{5,29},{6,4},{7,31},{8,14},{9,1},{... | collective-permute-start | bytes 786440 | tf_op jit(solution)/shard_map/ppermute | solution.py:236
  16.8 1.8 %collective-permute-done.4.refs_6_ = bf16[2,128,512]{2,1,0:T(8,128)(2,1)S(1)} collective-permute-done((bf16[2,128,512]{2,1,0:T(8,128)(2,1)S(1)}, bf16[2,128,512]{2,1,0:T(8,128)(2,1)S(1)}, u32[]{:S(2)}, u32[]{:S(2)}) %collective-permute-start.4) | collective-permute-done | bytes 262176 | tf_op jit(solution)/shard_map/ppermute | solution.py:236
  18.6 1.6 %collective-permute-start.14 = (bf16[2,128,512]{2,1,0:T(8,128)(2,1)S(1)}, bf16[2,128,512]{2,1,0:T(8,128)(2,1)S(1)}, u32[]{:S(2)}, u32[]{:S(2)}) collective-permute-start(bf16[2,128,512]{2,1,0:T(8,128)(2,1)S(1)} %collective-permute-done.4.refs_6_), channel_id=1, source_target_pairs={{0,1},{1,0},{2,3},{3,2},{4,5},{5,4},{6,7},{7,6},{8,9},{9,8},{10,11... | collective-permute-start | bytes 786440 | tf_op jit(solution)/shard_map/ppermute | solution.py:236
  20.2 1.6 %collective-permute-start.5 = (bf16[2,128,512]{2,1,0:T(8,128)(2,1)S(1)}, bf16[2,128,512]{2,1,0:T(8,128)(2,1)S(1)}, u32[]{:S(2)}, u32[]{:S(2)}) collective-permute-start(bf16[2,128,512]{2,1,0:T(8,128)(2,1)S(1)} %collective-permute-done.4.refs_6_), channel_id=1, source_target_pairs={{0,2},{1,9},{2,4},{3,11},{4,6},{5,13},{6,0},{7,15},{8,10},{9,17},{... | collective-permute-start | bytes 786440 | tf_op jit(solution)/shard_map/ppermute | solution.py:236
  21.9 2.7 %collective-permute-start.6 = (bf16[2,128,512]{2,1,0:T(8,128)(2,1)S(1)}, bf16[2,128,512]{2,1,0:T(8,128)(2,1)}, u32[]{:S(2)}, u32[]{:S(2)}) collective-permute-start(bf16[2,128,512]{2,1,0:T(8,128)(2,1)S(1)} %collective-permute-done.3.refs_3_), channel_id=1, source_target_pairs={{0,6},{1,25},{2,0},{3,27},{4,2},{5,29},{6,4},{7,31},{8,14},{9,1},{... | collective-permute-start | bytes 786440 | tf_op jit(solution)/shard_map/ppermute | solution.py:236
  24.6 1.0 copy-done.1
  26.4 8.2 %all-to-all-start = ((bf16[32,40,128]{2,1,0:T(8,128)(2,1)}), bf16[32,40,128]{2,1,0:T(8,128)(2,1)S(1)}, u32[]{:S(2)}, u32[]{:S(2)}) async-start(bf16[32,40,128]{2,1,0:T(8,128)(2,1)} %bitcast.2), calls=%async_computation | async-start | bytes 655360 | tf_op jit(solution)/shard_map/all_to_all | solution.py:270
  35.9 8.2 %all-to-all-done.refs_16_.got = bf16[32,40,128]{2,1,0:T(8,128)(2,1)S(1)} async-done(((bf16[32,40,128]{2,1,0:T(8,128)(2,1)}), bf16[32,40,128]{2,1,0:T(8,128)(2,1)S(1)}, u32[]{:S(2)}, u32[]{:S(2)}) %all-to-all-start) | async-done | bytes 327712 | tf_op jit(solution)/shard_map/all_to_all | solution.py:270
  44.2 1.4 %shard_map.66 = bf16[40,1024]{1,0:T(8,128)(2,1)S(1)} custom-call(bf16[2,128,512]{2,1,0:T(8,128)(2,1)S(1)} %pad_maximum_fusion.refs_0_, bf16[2,128,512]{2,1,0:T(8,128)(2,1)S(1)} %collective-permute-done.1.refs_1_, bf16[2,128,512]{2,1,0:T(8,128)(2,1)S(1)} %collective-permute-done.2.refs_2_, bf16[2,128,512]{2,1,0:T(8,128)(2,1)S(1)} %collective-permute-done.3.refs_3_, ...), custom_call_target="tpu_custom_call" | custom-call | tf_op jit(solution)/shard_map/pallas_call | solution.py:276
  46.3 1.0 %shard_map.68 = (bf16[1024,1024]{1,0:T(8,128)(2,1)S(1)}, bf16[1024,1024]{1,0:T(8,128)(2,1)S(1)}) custom-call(s32[1,1024]{1,0:T(1,128)S(1)} %copy-done.2), custom_call_target="tpu_custom_call" | custom-call | tf_op jit(solution)/shard_map/pallas_call | solution.py:272
  47.3 5.5 %shard_map.67 = (bf16[32,128,512]{2,1,0:T(8,128)(2,1)S(1)}, f32[40,512]{1,0:T(8,128)S(1)}, f32[40,1024]{1,0:T(8,128)S(1)}, bf16[1024,512]{1,0:T(8,128)(2,1)S(1)}) custom-call(bf16[2,128,512]{2,1,0:T(8,128)(2,1)S(1)} %pad_maximum_fusion.refs_0_, bf16[2,128,512]{2,1,0:T(8,128)(2,1)S(1)} %collective-permute-done.1.refs_1_, ...), custom_call_target="tpu_custom_call" | custom-call | tf_op jit(solution)/shard_map/pallas_call | solution.py:278
  52.8 1.1 %shard_map.69 = bf16[40,1024]{1,0:T(8,128)(2,1)S(1)} custom-call(bf16[40,1024]{1,0:T(8,128)(2,1)S(1)} %collective-permute-done.16.came.c1, f32[40,1024]{1,0:T(8,128)S(1)} %get-tuple-element.13.first, bf16[1024,512]{1,0:T(8,128)(2,1)S(1)} %get-tuple-element.14.gath, bf16[1,512,512]{2,1,0:T(8,128)(2,1)S(1)} %copy-done, ...), custom_call_target="tpu_custom_call" | custom-call | tf_op jit(solution)/shard_map/pallas_call | solution.py:289
  54.6 2.1 %shard_map.70 = (bf16[1024,512]{1,0:T(8,128)(2,1)S(1)}, bf16[1024,1024]{1,0:T(8,128)(2,1)S(1)}) custom-call(s32[1,1024]{1,0:T(1,128)S(1)} %copy-done.2, bf16[1024,512]{1,0:T(8,128)(2,1)S(1)} %get-tuple-element.14.gath, bf16[32,128,512]{2,1,0:T(8,128)(2,1)S(1)} %get-tuple-element.15.eff, bf16[1,512,512]{2,1,0:T(8,128)(2,1)S(1)} %copy-done), custom_call_target="tpu_custom_call" | custom-call | tf_op jit(solution)/shard_map/pallas_call | solution.py:293
  61.9 1.3 %collective-permute-start.22 = (bf16[40,1024]{1,0:T(8,128)(2,1)S(1)}, bf16[40,1024]{1,0:T(8,128)(2,1)S(1)}, u32[]{:S(2)}, u32[]{:S(2)}) collective-permute-start(bf16[40,1024]{1,0:T(8,128)(2,1)S(1)} %fusion.4), channel_id=1, source_target_pairs={{192,224},{193,225},{194,226},{195,227},{196,228},{197,229},{198,2... | collective-permute-start | bytes 245768 | tf_op jit(solution)/shard_map/ppermute | solution.py:301
  63.2 16.3 %collective-permute-done.22.c7 = bf16[40,1024]{1,0:T(8,128)(2,1)S(1)} collective-permute-done((bf16[40,1024]{1,0:T(8,128)(2,1)S(1)}, bf16[40,1024]{1,0:T(8,128)(2,1)S(1)}, u32[]{:S(2)}, u32[]{:S(2)}) %collective-permute-start.22) | collective-permute-done | bytes 81952 | tf_op jit(solution)/shard_map/ppermute | solution.py:301
  79.5 2.3 %shard_map.71 = bf16[32,40,128]{2,1,0:T(8,128)(2,1)S(1)} custom-call(bf16[40,1024]{1,0:T(8,128)(2,1)S(1)} %collective-permute-done.16.came.c1, bf16[40,1024]{1,0:T(8,128)(2,1)S(1)} %collective-permute-done.17.c2, bf16[40,1024]{1,0:T(8,128)(2,1)S(1)} %collective-permute-done.18.c3, bf16[40,1024]{1,0:T(8,128)(2,1)S(1)} %collective-permute-done.19.c4, ...), custom_call_target="tpu_custom_call" | custom-call | tf_op jit(solution)/shard_map/pallas_call | solution.py:303
  81.8 18.0 %all_to_all.10 = bf16[32,40,128]{2,1,0:T(8,128)(2,1)S(1)} all-to-all(bf16[32,40,128]{2,1,0:T(8,128)(2,1)S(1)} %shard_map.71), channel_id=1, replica_groups=mesh['front'=8,'row'=32] {'row'}, dimensions={0} | all-to-all | bytes 655360 | tf_op jit(solution)/shard_map/all_to_all | solution.py:306
  (46 shorter events, 10.6 us)
Async XLA Ops:
  1.7 4.4 %collective-permute-start = (bf16[128,512]{1,0:T(8,128)(2,1)}, bf16[128,512]{1,0:T(8,128)(2,1)S(1)}, u32[]{:S(2)}, u32[]{:S(2)}) collective-permute-start(bf16[128,512]{1,0:T(8,128)(2,1)} %shard_map.64), channel_id=1, source_target_pairs={{0,8},{1,3},{2,10},{3,1},{4,12},{5,7},{6,14},{7,5},{8,0},{9,11},{1... | collective-permute-start | bytes 393224 | tf_op jit(solution)/shard_map/ppermute | solution.py:236
  7.1 7.6 %collective-permute-start.1 = (bf16[2,128,512]{2,1,0:T(8,128)(2,1)S(1)}, bf16[2,128,512]{2,1,0:T(8,128)(2,1)S(1)}, u32[]{:S(2)}, u32[]{:S(2)}) collective-permute-start(bf16[2,128,512]{2,1,0:T(8,128)(2,1)S(1)} %pad_maximum_fusion.refs_0_), channel_id=1, source_target_pairs={{0,24},{1,7},{2,26},{3,5},{4,28},{5,3},{6,30},{7,1},{8,16},{9,15},... | collective-permute-start | bytes 786440 | tf_op jit(solution)/shard_map/ppermute | solution.py:236
  9.9 8.7 %collective-permute-start.4 = (bf16[2,128,512]{2,1,0:T(8,128)(2,1)S(1)}, bf16[2,128,512]{2,1,0:T(8,128)(2,1)S(1)}, u32[]{:S(2)}, u32[]{:S(2)}) collective-permute-start(bf16[2,128,512]{2,1,0:T(8,128)(2,1)S(1)} %pad_maximum_fusion.refs_0_), channel_id=1, source_target_pairs={{0,2},{1,9},{2,4},{3,11},{4,6},{5,13},{6,0},{7,15},{8,10},{9,17},{... | collective-permute-start | bytes 786440 | tf_op jit(solution)/shard_map/ppermute | solution.py:236
  11.1 10.7 %collective-permute-start.2 = (bf16[2,128,512]{2,1,0:T(8,128)(2,1)S(1)}, bf16[2,128,512]{2,1,0:T(8,128)(2,1)S(1)}, u32[]{:S(2)}, u32[]{:S(2)}) collective-permute-start(bf16[2,128,512]{2,1,0:T(8,128)(2,1)S(1)} %pad_maximum_fusion.refs_0_), channel_id=1, source_target_pairs={{0,6},{1,25},{2,0},{3,27},{4,2},{5,29},{6,4},{7,31},{8,14},{9,1},{... | collective-permute-start | bytes 786440 | tf_op jit(solution)/shard_map/ppermute | solution.py:236
  12.6 9.2 %collective-permute-start.8 = (bf16[2,128,512]{2,1,0:T(8,128)(2,1)S(1)}, bf16[2,128,512]{2,1,0:T(8,128)(2,1)S(1)}, u32[]{:S(2)}, u32[]{:S(2)}) collective-permute-start(bf16[2,128,512]{2,1,0:T(8,128)(2,1)S(1)} %pad_maximum_fusion.refs_0_), channel_id=1, source_target_pairs={{0,1},{1,0},{2,3},{3,2},{4,5},{5,4},{6,7},{7,6},{8,9},{9,8},{10,11... | collective-permute-start | bytes 786440 | tf_op jit(solution)/shard_map/ppermute | solution.py:236
  14.7 7.2 %collective-permute-start.3 = (bf16[2,128,512]{2,1,0:T(8,128)(2,1)S(1)}, bf16[2,128,512]{2,1,0:T(8,128)(2,1)S(1)}, u32[]{:S(2)}, u32[]{:S(2)}) collective-permute-start(bf16[2,128,512]{2,1,0:T(8,128)(2,1)S(1)} %collective-permute-done.1.refs_1_), channel_id=1, source_target_pairs={{0,6},{1,25},{2,0},{3,27},{4,2},{5,29},{6,4},{7,31},{8,14},{9,1},{... | collective-permute-start | bytes 786440 | tf_op jit(solution)/shard_map/ppermute | solution.py:236
  18.6 15.9 %collective-permute-start.14 = (bf16[2,128,512]{2,1,0:T(8,128)(2,1)S(1)}, bf16[2,128,512]{2,1,0:T(8,128)(2,1)S(1)}, u32[]{:S(2)}, u32[]{:S(2)}) collective-permute-start(bf16[2,128,512]{2,1,0:T(8,128)(2,1)S(1)} %collective-permute-done.4.refs_6_), channel_id=1, source_target_pairs={{0,1},{1,0},{2,3},{3,2},{4,5},{5,4},{6,7},{7,6},{8,9},{9,8},{10,11... | collective-permute-start | bytes 786440 | tf_op jit(solution)/shard_map/ppermute | solution.py:236
  20.2 14.7 %collective-permute-start.5 = (bf16[2,128,512]{2,1,0:T(8,128)(2,1)S(1)}, bf16[2,128,512]{2,1,0:T(8,128)(2,1)S(1)}, u32[]{:S(2)}, u32[]{:S(2)}) collective-permute-start(bf16[2,128,512]{2,1,0:T(8,128)(2,1)S(1)} %collective-permute-done.4.refs_6_), channel_id=1, source_target_pairs={{0,2},{1,9},{2,4},{3,11},{4,6},{5,13},{6,0},{7,15},{8,10},{9,17},{... | collective-permute-start | bytes 786440 | tf_op jit(solution)/shard_map/ppermute | solution.py:236
  21.8 13.4 %collective-permute-start.10 = (bf16[2,128,512]{2,1,0:T(8,128)(2,1)S(1)}, bf16[2,128,512]{2,1,0:T(8,128)(2,1)S(1)}, u32[]{:S(2)}, u32[]{:S(2)}) collective-permute-start(bf16[2,128,512]{2,1,0:T(8,128)(2,1)S(1)} %collective-permute-done.2.refs_2_), channel_id=1, source_target_pairs={{0,1},{1,0},{2,3},{3,2},{4,5},{5,4},{6,7},{7,6},{8,9},{9,8},{10,11... | collective-permute-start | bytes 786440 | tf_op jit(solution)/shard_map/ppermute | solution.py:236
  21.8 13.6 %collective-permute-start.7 = (bf16[2,128,512]{2,1,0:T(8,128)(2,1)S(1)}, bf16[2,128,512]{2,1,0:T(8,128)(2,1)S(1)}, u32[]{:S(2)}, u32[]{:S(2)}) collective-permute-start(bf16[2,128,512]{2,1,0:T(8,128)(2,1)S(1)} %collective-permute-done.1.refs_1_), channel_id=1, source_target_pairs={{0,2},{1,9},{2,4},{3,11},{4,6},{5,13},{6,0},{7,15},{8,10},{9,17},{... | collective-permute-start | bytes 786440 | tf_op jit(solution)/shard_map/ppermute | solution.py:236
  21.9 13.8 %collective-permute-start.6 = (bf16[2,128,512]{2,1,0:T(8,128)(2,1)S(1)}, bf16[2,128,512]{2,1,0:T(8,128)(2,1)}, u32[]{:S(2)}, u32[]{:S(2)}) collective-permute-start(bf16[2,128,512]{2,1,0:T(8,128)(2,1)S(1)} %collective-permute-done.3.refs_3_), channel_id=1, source_target_pairs={{0,6},{1,25},{2,0},{3,27},{4,2},{5,29},{6,4},{7,31},{8,14},{9,1},{... | collective-permute-start | bytes 786440 | tf_op jit(solution)/shard_map/ppermute | solution.py:236
  26.4 17.8 %all-to-all-start = ((bf16[32,40,128]{2,1,0:T(8,128)(2,1)}), bf16[32,40,128]{2,1,0:T(8,128)(2,1)S(1)}, u32[]{:S(2)}, u32[]{:S(2)}) async-start(bf16[32,40,128]{2,1,0:T(8,128)(2,1)} %bitcast.2), calls=%async_computation | async-start | bytes 655360 | tf_op jit(solution)/shard_map/all_to_all | solution.py:270
  34.6 9.6 %collective-permute-start.9 = (bf16[2,128,512]{2,1,0:T(8,128)(2,1)S(1)}, bf16[2,128,512]{2,1,0:T(8,128)(2,1)}, u32[]{:S(2)}, u32[]{:S(2)}) collective-permute-start(bf16[2,128,512]{2,1,0:T(8,128)(2,1)S(1)} %collective-permute-done.1.refs_1_), channel_id=1, source_target_pairs={{0,1},{1,0},{2,3},{3,2},{4,5},{5,4},{6,7},{7,6},{8,9},{9,8},{10,11... | collective-permute-start | bytes 786440 | tf_op jit(solution)/shard_map/ppermute | solution.py:236
  34.9 9.3 %collective-permute-start.11 = (bf16[2,128,512]{2,1,0:T(8,128)(2,1)S(1)}, bf16[2,128,512]{2,1,0:T(8,128)(2,1)}, u32[]{:S(2)}, u32[]{:S(2)}) collective-permute-start(bf16[2,128,512]{2,1,0:T(8,128)(2,1)S(1)} %collective-permute-done.3.refs_3_), channel_id=1, source_target_pairs={{0,1},{1,0},{2,3},{3,2},{4,5},{5,4},{6,7},{7,6},{8,9},{9,8},{10,11... | collective-permute-start | bytes 786440 | tf_op jit(solution)/shard_map/ppermute | solution.py:236
  35.2 9.0 %collective-permute-start.12 = (bf16[2,128,512]{2,1,0:T(8,128)(2,1)S(1)}, bf16[2,128,512]{2,1,0:T(8,128)(2,1)}, u32[]{:S(2)}, u32[]{:S(2)}) collective-permute-start(bf16[2,128,512]{2,1,0:T(8,128)(2,1)S(1)} %collective-permute-done.5.refs_4_), channel_id=1, source_target_pairs={{0,1},{1,0},{2,3},{3,2},{4,5},{5,4},{6,7},{7,6},{8,9},{9,8},{10,11... | collective-permute-start | bytes 786440 | tf_op jit(solution)/shard_map/ppermute | solution.py:236
  35.4 8.8 %collective-permute-start.15 = (bf16[2,128,512]{2,1,0:T(8,128)(2,1)S(1)}, bf16[2,128,512]{2,1,0:T(8,128)(2,1)}, u32[]{:S(2)}, u32[]{:S(2)}) collective-permute-start(bf16[2,128,512]{2,1,0:T(8,128)(2,1)S(1)} %collective-permute-done.7.refs_7_), channel_id=1, source_target_pairs={{0,1},{1,0},{2,3},{3,2},{4,5},{5,4},{6,7},{7,6},{8,9},{9,8},{10,11... | collective-permute-start | bytes 786440 | tf_op jit(solution)/shard_map/ppermute | solution.py:236
  35.7 8.5 %collective-permute-start.13 = (bf16[2,128,512]{2,1,0:T(8,128)(2,1)}, bf16[2,128,512]{2,1,0:T(8,128)(2,1)}, u32[]{:S(2)}, u32[]{:S(2)}) collective-permute-start(bf16[2,128,512]{2,1,0:T(8,128)(2,1)} %collective-permute-done.6.refs_5_), channel_id=1, source_target_pairs={{0,1},{1,0},{2,3},{3,2},{4,5},{5,4},{6,7},{7,6},{8,9},{9,8},{10,11... | collective-permute-start | bytes 786440 | tf_op jit(solution)/shard_map/ppermute | solution.py:236
  45.6 7.2 %collective-permute-start.16 = (bf16[40,1024]{1,0:T(8,128)(2,1)S(1)}, bf16[40,1024]{1,0:T(8,128)(2,1)S(1)}, u32[]{:S(2)}, u32[]{:S(2)}) collective-permute-start(bf16[40,1024]{1,0:T(8,128)(2,1)S(1)} %shard_map.66), channel_id=1, source_target_pairs={{0,32},{1,33},{2,34},{3,35},{4,36},{5,37},{6,38},{7,39},{8,40},{9,... | collective-permute-start | bytes 245768 | tf_op jit(solution)/shard_map/ppermute | solution.py:277
  53.9 2.8 %collective-permute-start.17 = (bf16[40,1024]{1,0:T(8,128)(2,1)S(1)}, bf16[40,1024]{1,0:T(8,128)(2,1)S(1)}, u32[]{:S(2)}, u32[]{:S(2)}) collective-permute-start(bf16[40,1024]{1,0:T(8,128)(2,1)S(1)} %shard_map.69), channel_id=1, source_target_pairs={{32,64},{33,65},{34,66},{35,67},{36,68},{37,69},{38,70},{39,71},{4... | collective-permute-start | bytes 245768 | tf_op jit(solution)/shard_map/ppermute | solution.py:292
  57.2 0.7 collective-permute-start.18
  58.4 0.7 collective-permute-start.19
  59.6 0.7 collective-permute-start.20
  60.8 0.7 collective-permute-start.21
  61.9 17.6 %collective-permute-start.22 = (bf16[40,1024]{1,0:T(8,128)(2,1)S(1)}, bf16[40,1024]{1,0:T(8,128)(2,1)S(1)}, u32[]{:S(2)}, u32[]{:S(2)}) collective-permute-start(bf16[40,1024]{1,0:T(8,128)(2,1)S(1)} %fusion.4), channel_id=1, source_target_pairs={{192,224},{193,225},{194,226},{195,227},{196,228},{197,229},{198,2... | collective-permute-start | bytes 245768 | tf_op jit(solution)/shard_map/ppermute | solution.py:301
  (3 other events, 56.9 us)

commit v3 on v2

--- a/solution.py
+++ b/solution.py
@@ -36,14 +36,6 @@
                 to_x, to_y = (step(x), y) if along_x else (x, step(y))
                 pairs.append((place(x, y, core), place(to_x, to_y, core)))
     return pairs
-
-
-def near_mate(p):
-    return p ^ 1
-
-
-def far_mate(p):
-    return p + 1 if p % 2 else p - 1
 
 
 SWAP = [(place(x, y, c), place(x, y, 1 - c)) for x in range(SIDE) for y in range(SIDE) for c in range(2)]
@@ -92,15 +84,10 @@
 def slots(row, sibling):
     x, y, core = row // (2 * SIDE), (row // 2) % SIDE, row % 2
     who = 1 - core if sibling else core
-    one, two = jnp.where(who == 0, x, y), jnp.where(who == 0, y, x)
-    near = one + 1 - 2 * (one % 2)
-    far = (one + SIDE - 1 + 2 * (one % 2)) % SIDE
-    beyond = far + 1 - 2 * (far % 2)
     for j in range(SIDE):
-        for k, held in enumerate((one, near, far, beyond)):
-            other = (two + j) % SIDE
-            at_x, at_y = jnp.where(who == 0, held, other), jnp.where(who == 0, other, held)
-            yield j, k, (at_x * SIDE + at_y) * 2 + who
+        for k in range(SIDE):
+            dx, dy = jnp.where(who == 0, k, j), jnp.where(who == 0, j, k)
+            yield j, k, (((x + dx) % SIDE) * SIDE + (y + dy) % SIDE) * 2 + who
 
 
 def product(row, mine, theirs, got, eff, acc):
@@ -148,7 +135,8 @@
 
 
 def base_kernel(*refs):
-    mine, theirs, (got, coeffs, carry, eff, base, first, gath, wide) = refs[:8], refs[8:16], refs[16:]
+    mine, theirs, own = refs[:8], refs[8:16], refs[16:]
+    got, coeffs, carry, eff, base, first, gath, order, spread, wide = own
     acc = product(lax.axis_index("row"), mine, theirs, got, eff, jnp.zeros(base.shape, F32))
     m = mm(acc.astype(BF), coeffs[0])
     base[...] = m
@@ -169,14 +157,30 @@
                 wide[k, pl.ds(b + h, EACH, stride=ROWS), :] = tile
     for k in range(WIDTH // 128):
         gath[:, k * 128 : (k + 1) * 128] = wide[k].astype(BF)
+    fill_order(order, CARRIED - QUARTER)
+    fill_spread(spread, offsets, TAIL)
+
+
+def fill_order(order, start):
+    for r in range(0, CARRIED, 128):
+        down = r + lax.broadcasted_iota(I32, (128, order.shape[1]), 0)
+        right = start + lax.broadcasted_iota(I32, (128, order.shape[1]), 1)
+        order[r : r + 128, :] = ((right % EACH) * ROWS + right // EACH == down).astype(F32).astype(BF)
+
+
+def fill_spread(spread, offsets, start):
+    lane = lax.broadcasted_iota(I32, (EACH, 8 * SPAN), 1)
+    for b in range(start, ROWS):
+        where = offsets[:, b : b + 1] + (b % 8) * SPAN
+        at = (b - start) * EACH
+        spread[at : at + EACH, :] = (where == lane).astype(F32).astype(BF)
 
 
 def second_kernel(came, first, gath, coeffs, eff, order, spread, sent):
     cin = came[...]
     w = mm(cin, gath[...]).astype(BF)
     t = mm(w, coeffs[0]).astype(BF)
-    placed = mm(cin, order[:, CARRIED - QUARTER :]).astype(BF)
-    moved = mm(placed, spread[CARRIED - QUARTER :, :])
+    moved = mm(mm(cin, order[...]).astype(BF), spread[...])
     for b in range(TAIL, ROWS, 2):
         at = slice((b - TAIL) * SPAN, (b - TAIL + 2) * SPAN)
         down = mm(t, eff[b : b + 2].reshape(2 * SPAN, WIDTH), ((1,), (1,)))
@@ -202,15 +206,8 @@
 
 
 def table_kernel(carry, order, spread):
-    offsets = unfold(carry[...])
-    for r in range(0, CARRIED, 128):
-        down = r + lax.broadcasted_iota(I32, (128, CARRIED), 0)
-        right = lax.broadcasted_iota(I32, (128, CARRIED), 1)
-        order[r : r + 128, :] = ((right % EACH) * ROWS + right // EACH == down).astype(F32).astype(BF)
-    lane = lax.broadcasted_iota(I32, (EACH, 8 * SPAN), 1)
-    for b in range(ROWS):
-        where = offsets[:, b : b + 1] + (b % 8) * SPAN
-        spread[b * EACH : (b + 1) * EACH, :] = (where == lane).astype(F32).astype(BF)
+    fill_order(order, 0)
+    fill_spread(spread, unfold(carry[...]), 0)
 
 
 def last_kernel(c1, c2, c3, c4, c5, c6, c7, base, turn, order, spread, got, eff, out):
@@ -234,12 +231,17 @@
 
 def gather_rows(own):
     pp = lambda value, pairs: lax.ppermute(value, "row", pairs)
+    half = own.shape[0] // 2
+    along, back = moves(False, lambda p: p + 1), moves(False, lambda p: p - 1)
     up, down = moves(True, lambda p: p + 1), moves(True, lambda p: p - 1)
-    mate = pp(own, moves(False, near_mate))
-    near = jnp.stack([own, mate])
-    rest = pp(near, moves(False, far_mate))
+    right = pp(own, back)
+    left = pp(own, along)
+    far_a = pp(left[:half], along)
+    far_b = pp(right[half:], back)
+    near = jnp.stack([own, right])
     near_left = pp(near, up)
     near_right = pp(near, down)
+    rest = jnp.stack([jnp.concatenate([far_a, far_b]), left])
     rest_right = pp(rest, down)
     rest_left = pp(rest, up)
     near_far = pp(near_left, up)
@@ -275,19 +277,21 @@
 
     sent = call(first_kernel, shape((part, CARRIED)), [VMEM] * 18)(*parts, got, block_coeffs)
     came = [lax.ppermute(sent, "front", [(0, 1)])]
-    eff, base, first, gath = call(
+    eff, base, first, gath, low_order, low_spread = call(
         base_kernel,
         (
             shape((ROWS, SPAN, WIDTH)),
             shape((part, WIDTH), F32),
             shape((part, CARRIED), F32),
             shape((CARRIED, WIDTH)),
+            shape((CARRIED, QUARTER)),
+            shape((QUARTER, 8 * SPAN)),
         ),
         [VMEM] * 19,
         scratch=[pltpu.VMEM((WIDTH // 128, CARRIED, 128), F32)],
     )(*parts, got, block_coeffs, carry_map)
     sent = call(second_kernel, shape((part, CARRIED)), [VMEM] * 7)(
-        came[0], first, gath, block_coeffs, eff, order, spread
+        came[0], first, gath, block_coeffs, eff, low_order, low_spread
     )
     came.append(lax.ppermute(sent, "front", [(1, 2)]))
     turn, hop = call(

time: 101 us -> 98.1 us (0.971)
  starting transfers between devices: 31.8 us -> 29.1 us
    all_to_all x1, starting transfers between devices: 8.16 us -> 5.03 us  [work(): lax.all_to_all(pieces.reshape(ROWS, part, SPAN), 'row', 0, 0, tiled=True)]
    ppermute x16 -> x18, waiting for transfers between devices: 4.87 us -> 5.4 us  [gather_rows(): pp = lambda value, pairs: lax.ppermute(value, 'row', pairs)]
    ppermute x16 -> x18, starting transfers between devices: 18.4 us -> 18.8 us  [gather_rows(): pp = lambda value, pairs: lax.ppermute(value, 'row', pairs)]
  transfers between devices with their start and end apart: 24 -> 26, of which waited for: 4 -> 5; matrix products, arithmetic and copies ran while one was open for 0% -> 1% of each run, Pallas kernels for 9% -> 10%
where the time goes in v3:
time: 98.1 us; the launch traced here: 97.7 us
  starting transfers between devices  29.1 us (30%)
  waiting for transfers between devices  28.9 us (29%)
  blocking collectives  18 us (18%)
  Pallas kernels  16.1 us (16%)
  matrix products  2.41 us (2%)
  local copies, waits for them, and re-layouts  1.9 us (2%)
    ppermute x18, starting transfers between devices, gather_rows(): pp = lambda value, pairs: lax.ppermute(value, 'row', pairs)  18.8 us
    all_to_all x1, blocking collectives, work(): home = lax.all_to_all(out, 'row', 0, 0, tiled=True)  18 us
    ppermute x5, waiting for transfers between devices, work(): came.append(lax.ppermute(sent, 'front', [(step - 1, step)]))  15.3 us
    all_to_all x1, waiting for transfers between devices, work(): lax.all_to_all(pieces.reshape(ROWS, part, SPAN), 'row', 0, 0, tiled=True)  8.24 us
    pallas_call x1, Pallas kernels, work(): call(base_kernel, (shape((ROWS, SPAN, WIDTH)), shape((part, WIDTH), F32),...  5.65 us
    ppermute x18, waiting for transfers between devices, gather_rows(): pp = lambda value, pairs: lax.ppermute(value, 'row', pairs)  5.4 us
    all_to_all x1, starting transfers between devices, work(): lax.all_to_all(pieces.reshape(ROWS, part, SPAN), 'row', 0, 0, tiled=True)  5.03 us
    ppermute x5, starting transfers between devices, work(): came.append(lax.ppermute(sent, 'front', [(step - 1, step)]))  3.96 us
  transfers between devices with their start and end apart: 26, of which 5 were waited for; matrix products, arithmetic and copies ran while one was open for 1% of the time, Pallas kernels for 10%

profile of v3, /device:TPU:225, one launch (start us, length us, event | category | flops | bytes accessed | tf_op | source)
XLA Modules:
  0.0 97.7 jit_solution(8194688138145655643)
XLA Ops:
  0.0 1.7 %shard_map.64 = bf16[128,512]{1,0:T(8,128)(2,1)} custom-call(s32[1,1,4]{2,1,0:T(1,128)} %mask.1, s32[1,4]{1,0:T(1,128)} %starts.1, bf16[1,128,512]{2,1,0:T(8,128)(2,1)} %refl.1), custom_call_target="tpu_custom_call" | custom-call | tf_op jit(solution)/shard_map/pallas_call | solution.py:260
  1.7 1.4 %collective-permute-start.1 = (bf16[128,512]{1,0:T(8,128)(2,1)}, bf16[128,512]{1,0:T(8,128)(2,1)S(1)}, u32[]{:S(2)}, u32[]{:S(2)}) collective-permute-start(bf16[128,512]{1,0:T(8,128)(2,1)} %shard_map.64), channel_id=1, source_target_pairs={{0,8},{1,3},{2,10},{3,5},{4,12},{5,7},{6,14},{7,1},{8,16},{9,11},{... | collective-permute-start | bytes 393224 | tf_op jit(solution)/shard_map/ppermute | solution.py:233
  3.1 1.5 %collective-permute-start = (bf16[128,512]{1,0:T(8,128)(2,1)}, bf16[128,512]{1,0:T(8,128)(2,1)S(1)}, u32[]{:S(2)}, u32[]{:S(2)}) collective-permute-start(bf16[128,512]{1,0:T(8,128)(2,1)} %shard_map.64), channel_id=1, source_target_pairs={{0,24},{1,7},{2,26},{3,1},{4,28},{5,3},{6,30},{7,5},{8,0},{9,15},{... | collective-permute-start | bytes 393224 | tf_op jit(solution)/shard_map/ppermute | solution.py:233
  4.6 2.8 %collective-permute-done.1 = bf16[128,512]{1,0:T(8,128)(2,1)S(1)} collective-permute-done((bf16[128,512]{1,0:T(8,128)(2,1)}, bf16[128,512]{1,0:T(8,128)(2,1)S(1)}, u32[]{:S(2)}, u32[]{:S(2)}) %collective-permute-start.1) | collective-permute-done | bytes 131104 | tf_op jit(solution)/shard_map/ppermute | solution.py:233
  7.4 2.7 %collective-permute-start.3 = (bf16[64,512]{1,0:T(8,128)(2,1)S(1)}, bf16[64,512]{1,0:T(8,128)(2,1)S(1)}, u32[]{:S(2)}, u32[]{:S(2)}) collective-permute-start(bf16[64,512]{1,0:T(8,128)(2,1)S(1)} %slice.9), channel_id=1, source_target_pairs={{0,24},{1,7},{2,26},{3,1},{4,28},{5,3},{6,30},{7,5},{8,0},{9,15},{... | collective-permute-start | bytes 196616 | tf_op jit(solution)/shard_map/ppermute | solution.py:233
  11.1 2.1 %collective-permute-start.10 = (bf16[2,128,512]{2,1,0:T(8,128)(2,1)S(1)}, bf16[2,128,512]{2,1,0:T(8,128)(2,1)S(1)}, u32[]{:S(2)}, u32[]{:S(2)}) collective-permute-start(bf16[2,128,512]{2,1,0:T(8,128)(2,1)S(1)} %pad_maximum_fusion.refs_0_), channel_id=1, source_target_pairs={{0,1},{1,0},{2,3},{3,2},{4,5},{5,4},{6,7},{7,6},{8,9},{9,8},{10,11... | collective-permute-start | bytes 786440 | tf_op jit(solution)/shard_map/ppermute | solution.py:233
  13.2 2.7 %collective-permute-start.4 = (bf16[2,128,512]{2,1,0:T(8,128)(2,1)S(1)}, bf16[2,128,512]{2,1,0:T(8,128)(2,1)S(1)}, u32[]{:S(2)}, u32[]{:S(2)}) collective-permute-start(bf16[2,128,512]{2,1,0:T(8,128)(2,1)S(1)} %pad_maximum_fusion.refs_0_), channel_id=1, source_target_pairs={{0,6},{1,25},{2,0},{3,27},{4,2},{5,29},{6,4},{7,31},{8,14},{9,1},{... | collective-permute-start | bytes 786440 | tf_op jit(solution)/shard_map/ppermute | solution.py:233
  16.0 2.4 %collective-permute-start.11 = (bf16[2,128,512]{2,1,0:T(8,128)(2,1)S(1)}, bf16[2,128,512]{2,1,0:T(8,128)(2,1)S(1)}, u32[]{:S(2)}, u32[]{:S(2)}) collective-permute-start(bf16[2,128,512]{2,1,0:T(8,128)(2,1)S(1)} %pad_maximum_fusion.1.refs_1_), channel_id=1, source_target_pairs={{0,1},{1,0},{2,3},{3,2},{4,5},{5,4},{6,7},{7,6},{8,9},{9,8},{10,11... | collective-permute-start | bytes 786440 | tf_op jit(solution)/shard_map/ppermute | solution.py:233
  18.5 1.5 %collective-permute-done.6.refs_6_ = bf16[2,128,512]{2,1,0:T(8,128)(2,1)S(1)} collective-permute-done((bf16[2,128,512]{2,1,0:T(8,128)(2,1)S(1)}, bf16[2,128,512]{2,1,0:T(8,128)(2,1)S(1)}, u32[]{:S(2)}, u32[]{:S(2)}) %collective-permute-start.6) | collective-permute-done | bytes 262176 | tf_op jit(solution)/shard_map/ppermute | solution.py:233
  19.9 0.9 collective-permute-start.16
  20.9 1.1 %collective-permute-done.5.refs_3_ = bf16[2,128,512]{2,1,0:T(8,128)(2,1)S(1)} collective-permute-done((bf16[2,128,512]{2,1,0:T(8,128)(2,1)S(1)}, bf16[2,128,512]{2,1,0:T(8,128)(2,1)S(1)}, u32[]{:S(2)}, u32[]{:S(2)}) %collective-permute-start.5) | collective-permute-done | bytes 262176 | tf_op jit(solution)/shard_map/ppermute | solution.py:233
  22.0 3.4 %collective-permute-start.8 = (bf16[2,128,512]{2,1,0:T(8,128)(2,1)S(1)}, bf16[2,128,512]{2,1,0:T(8,128)(2,1)}, u32[]{:S(2)}, u32[]{:S(2)}) collective-permute-start(bf16[2,128,512]{2,1,0:T(8,128)(2,1)S(1)} %collective-permute-done.5.refs_3_), channel_id=1, source_target_pairs={{0,6},{1,25},{2,0},{3,27},{4,2},{5,29},{6,4},{7,31},{8,14},{9,1},{... | collective-permute-start | bytes 786440 | tf_op jit(solution)/shard_map/ppermute | solution.py:233
  25.4 1.0 copy-done.1
  27.3 5.0 %all-to-all-start = ((bf16[32,40,128]{2,1,0:T(8,128)(2,1)}), bf16[32,40,128]{2,1,0:T(8,128)(2,1)S(1)}, u32[]{:S(2)}, u32[]{:S(2)}) async-start(bf16[32,40,128]{2,1,0:T(8,128)(2,1)} %bitcast.4), calls=%async_computation | async-start | bytes 655360 | tf_op jit(solution)/shard_map/all_to_all | solution.py:272
  33.8 8.2 %all-to-all-done.refs_16_.got = bf16[32,40,128]{2,1,0:T(8,128)(2,1)S(1)} async-done(((bf16[32,40,128]{2,1,0:T(8,128)(2,1)}), bf16[32,40,128]{2,1,0:T(8,128)(2,1)S(1)}, u32[]{:S(2)}, u32[]{:S(2)}) %all-to-all-start) | async-done | bytes 327712 | tf_op jit(solution)/shard_map/all_to_all | solution.py:272
  42.1 1.4 %shard_map.66 = bf16[40,1024]{1,0:T(8,128)(2,1)S(1)} custom-call(bf16[2,128,512]{2,1,0:T(8,128)(2,1)S(1)} %pad_maximum_fusion.refs_0_, bf16[2,128,512]{2,1,0:T(8,128)(2,1)S(1)} %pad_maximum_fusion.1.refs_1_, bf16[2,128,512]{2,1,0:T(8,128)(2,1)S(1)} %collective-permute-done.4.refs_2_, bf16[2,128,512]{2,1,0:T(8,128)(2,1)S(1)} %collective-permute-done.5.refs_3_, ...), custom_call_target="tpu_custom_call" | custom-call | tf_op jit(solution)/shard_map/pallas_call | solution.py:278
  44.1 5.7 %shard_map.67 = (bf16[32,128,512]{2,1,0:T(8,128)(2,1)S(1)}, f32[40,512]{1,0:T(8,128)S(1)}, f32[40,1024]{1,0:T(8,128)S(1)}, bf16[1024,512]{1,0:T(8,128)(2,1)S(1)}...) custom-call(bf16[2,128,512]{2,1,0:T(8,128)(2,1)S(1)} %pad_maximum_fusion.refs_0_, ...), custom_call_target="tpu_custom_call" | custom-call | tf_op jit(solution)/shard_map/pallas_call | solution.py:280
  49.8 1.1 %shard_map.68 = bf16[40,1024]{1,0:T(8,128)(2,1)S(1)} custom-call(bf16[40,1024]{1,0:T(8,128)(2,1)S(1)} %collective-permute-done.18.came.c1, f32[40,1024]{1,0:T(8,128)S(1)} %get-tuple-element.15.first, bf16[1024,512]{1,0:T(8,128)(2,1)S(1)} %get-tuple-element.16.gath, bf16[1,512,512]{2,1,0:T(8,128)(2,1)S(1)} %copy-done, ...), custom_call_target="tpu_custom_call" | custom-call | tf_op jit(solution)/shard_map/pallas_call | solution.py:293
  51.6 2.2 %shard_map.69 = (bf16[1024,512]{1,0:T(8,128)(2,1)S(1)}, bf16[1024,1024]{1,0:T(8,128)(2,1)S(1)}) custom-call(s32[1,1024]{1,0:T(1,128)S(1)} %copy-done.2, bf16[1024,512]{1,0:T(8,128)(2,1)S(1)} %get-tuple-element.16.gath, bf16[32,128,512]{2,1,0:T(8,128)(2,1)S(1)} %get-tuple-element.17.eff, bf16[1,512,512]{2,1,0:T(8,128)(2,1)S(1)} %copy-done), custom_call_target="tpu_custom_call" | custom-call | tf_op jit(solution)/shard_map/pallas_call | solution.py:297
  58.9 1.3 %collective-permute-start.24 = (bf16[40,1024]{1,0:T(8,128)(2,1)S(1)}, bf16[40,1024]{1,0:T(8,128)(2,1)S(1)}, u32[]{:S(2)}, u32[]{:S(2)}) collective-permute-start(bf16[40,1024]{1,0:T(8,128)(2,1)S(1)} %fusion.4), channel_id=1, source_target_pairs={{192,224},{193,225},{194,226},{195,227},{196,228},{197,229},{198,2... | collective-permute-start | bytes 245768 | tf_op jit(solution)/shard_map/ppermute | solution.py:305
  60.2 1.0 %shard_map.70 = (bf16[1024,1024]{1,0:T(8,128)(2,1)S(1)}, bf16[1024,1024]{1,0:T(8,128)(2,1)S(1)}) custom-call(s32[1,1024]{1,0:T(1,128)S(1)} %copy-done.2), custom_call_target="tpu_custom_call" | custom-call | tf_op jit(solution)/shard_map/pallas_call | solution.py:274
  61.2 15.3 %collective-permute-done.24.c7 = bf16[40,1024]{1,0:T(8,128)(2,1)S(1)} collective-permute-done((bf16[40,1024]{1,0:T(8,128)(2,1)S(1)}, bf16[40,1024]{1,0:T(8,128)(2,1)S(1)}, u32[]{:S(2)}, u32[]{:S(2)}) %collective-permute-start.24) | collective-permute-done | bytes 81952 | tf_op jit(solution)/shard_map/ppermute | solution.py:305
  76.5 2.3 %shard_map.71 = bf16[32,40,128]{2,1,0:T(8,128)(2,1)S(1)} custom-call(bf16[40,1024]{1,0:T(8,128)(2,1)S(1)} %collective-permute-done.18.came.c1, bf16[40,1024]{1,0:T(8,128)(2,1)S(1)} %collective-permute-done.19.c2, bf16[40,1024]{1,0:T(8,128)(2,1)S(1)} %collective-permute-done.20.c3, bf16[40,1024]{1,0:T(8,128)(2,1)S(1)} %collective-permute-done.21.c4, ...), custom_call_target="tpu_custom_call" | custom-call | tf_op jit(solution)/shard_map/pallas_call | solution.py:307
  78.8 18.0 %all_to_all.10 = bf16[32,40,128]{2,1,0:T(8,128)(2,1)S(1)} all-to-all(bf16[32,40,128]{2,1,0:T(8,128)(2,1)S(1)} %shard_map.71), channel_id=1, replica_groups=mesh['front'=8,'row'=32] {'row'}, dimensions={0} | all-to-all | bytes 655360 | tf_op jit(solution)/shard_map/all_to_all | solution.py:310
  (54 shorter events, 10.8 us)
Async XLA Ops:
  1.7 5.7 %collective-permute-start.1 = (bf16[128,512]{1,0:T(8,128)(2,1)}, bf16[128,512]{1,0:T(8,128)(2,1)S(1)}, u32[]{:S(2)}, u32[]{:S(2)}) collective-permute-start(bf16[128,512]{1,0:T(8,128)(2,1)} %shard_map.64), channel_id=1, source_target_pairs={{0,8},{1,3},{2,10},{3,5},{4,12},{5,7},{6,14},{7,1},{8,16},{9,11},{... | collective-permute-start | bytes 393224 | tf_op jit(solution)/shard_map/ppermute | solution.py:233
  3.1 4.3 %collective-permute-start = (bf16[128,512]{1,0:T(8,128)(2,1)}, bf16[128,512]{1,0:T(8,128)(2,1)S(1)}, u32[]{:S(2)}, u32[]{:S(2)}) collective-permute-start(bf16[128,512]{1,0:T(8,128)(2,1)} %shard_map.64), channel_id=1, source_target_pairs={{0,24},{1,7},{2,26},{3,1},{4,28},{5,3},{6,30},{7,5},{8,0},{9,15},{... | collective-permute-start | bytes 393224 | tf_op jit(solution)/shard_map/ppermute | solution.py:233
  7.4 8.5 %collective-permute-start.2 = (bf16[64,512]{1,0:T(8,128)(2,1)S(1)}, bf16[64,512]{1,0:T(8,128)(2,1)S(1)}, u32[]{:S(2)}, u32[]{:S(2)}) collective-permute-start(bf16[64,512]{1,0:T(8,128)(2,1)S(1)} %slice.8), channel_id=1, source_target_pairs={{0,8},{1,3},{2,10},{3,5},{4,12},{5,7},{6,14},{7,1},{8,16},{9,11},{... | collective-permute-start | bytes 196616 | tf_op jit(solution)/shard_map/ppermute | solution.py:233
  7.4 8.5 %collective-permute-start.3 = (bf16[64,512]{1,0:T(8,128)(2,1)S(1)}, bf16[64,512]{1,0:T(8,128)(2,1)S(1)}, u32[]{:S(2)}, u32[]{:S(2)}) collective-permute-start(bf16[64,512]{1,0:T(8,128)(2,1)S(1)} %slice.9), channel_id=1, source_target_pairs={{0,24},{1,7},{2,26},{3,1},{4,28},{5,3},{6,30},{7,5},{8,0},{9,15},{... | collective-permute-start | bytes 196616 | tf_op jit(solution)/shard_map/ppermute | solution.py:233
  11.1 7.4 %collective-permute-start.10 = (bf16[2,128,512]{2,1,0:T(8,128)(2,1)S(1)}, bf16[2,128,512]{2,1,0:T(8,128)(2,1)S(1)}, u32[]{:S(2)}, u32[]{:S(2)}) collective-permute-start(bf16[2,128,512]{2,1,0:T(8,128)(2,1)S(1)} %pad_maximum_fusion.refs_0_), channel_id=1, source_target_pairs={{0,1},{1,0},{2,3},{3,2},{4,5},{5,4},{6,7},{7,6},{8,9},{9,8},{10,11... | collective-permute-start | bytes 786440 | tf_op jit(solution)/shard_map/ppermute | solution.py:233
  13.2 6.7 %collective-permute-start.6 = (bf16[2,128,512]{2,1,0:T(8,128)(2,1)S(1)}, bf16[2,128,512]{2,1,0:T(8,128)(2,1)S(1)}, u32[]{:S(2)}, u32[]{:S(2)}) collective-permute-start(bf16[2,128,512]{2,1,0:T(8,128)(2,1)S(1)} %pad_maximum_fusion.refs_0_), channel_id=1, source_target_pairs={{0,2},{1,9},{2,4},{3,11},{4,6},{5,13},{6,0},{7,15},{8,10},{9,17},{... | collective-permute-start | bytes 786440 | tf_op jit(solution)/shard_map/ppermute | solution.py:233
  13.2 7.7 %collective-permute-start.4 = (bf16[2,128,512]{2,1,0:T(8,128)(2,1)S(1)}, bf16[2,128,512]{2,1,0:T(8,128)(2,1)S(1)}, u32[]{:S(2)}, u32[]{:S(2)}) collective-permute-start(bf16[2,128,512]{2,1,0:T(8,128)(2,1)S(1)} %pad_maximum_fusion.refs_0_), channel_id=1, source_target_pairs={{0,6},{1,25},{2,0},{3,27},{4,2},{5,29},{6,4},{7,31},{8,14},{9,1},{... | collective-permute-start | bytes 786440 | tf_op jit(solution)/shard_map/ppermute | solution.py:233
  15.9 6.1 %collective-permute-start.5 = (bf16[2,128,512]{2,1,0:T(8,128)(2,1)S(1)}, bf16[2,128,512]{2,1,0:T(8,128)(2,1)S(1)}, u32[]{:S(2)}, u32[]{:S(2)}) collective-permute-start(bf16[2,128,512]{2,1,0:T(8,128)(2,1)S(1)} %pad_maximum_fusion.1.refs_1_), channel_id=1, source_target_pairs={{0,6},{1,25},{2,0},{3,27},{4,2},{5,29},{6,4},{7,31},{8,14},{9,1},{... | collective-permute-start | bytes 786440 | tf_op jit(solution)/shard_map/ppermute | solution.py:233
  16.0 16.3 %collective-permute-start.11 = (bf16[2,128,512]{2,1,0:T(8,128)(2,1)S(1)}, bf16[2,128,512]{2,1,0:T(8,128)(2,1)S(1)}, u32[]{:S(2)}, u32[]{:S(2)}) collective-permute-start(bf16[2,128,512]{2,1,0:T(8,128)(2,1)S(1)} %pad_maximum_fusion.1.refs_1_), channel_id=1, source_target_pairs={{0,1},{1,0},{2,3},{3,2},{4,5},{5,4},{6,7},{7,6},{8,9},{9,8},{10,11... | collective-permute-start | bytes 786440 | tf_op jit(solution)/shard_map/ppermute | solution.py:233
  18.5 14.3 %collective-permute-start.9 = (bf16[2,128,512]{2,1,0:T(8,128)(2,1)S(1)}, bf16[2,128,512]{2,1,0:T(8,128)(2,1)S(1)}, u32[]{:S(2)}, u32[]{:S(2)}) collective-permute-start(bf16[2,128,512]{2,1,0:T(8,128)(2,1)S(1)} %pad_maximum_fusion.1.refs_1_), channel_id=1, source_target_pairs={{0,2},{1,9},{2,4},{3,11},{4,6},{5,13},{6,0},{7,15},{8,10},{9,17},{... | collective-permute-start | bytes 786440 | tf_op jit(solution)/shard_map/ppermute | solution.py:233
  19.9 13.0 %collective-permute-start.16 = (bf16[2,128,512]{2,1,0:T(8,128)(2,1)S(1)}, bf16[2,128,512]{2,1,0:T(8,128)(2,1)S(1)}, u32[]{:S(2)}, u32[]{:S(2)}) collective-permute-start(bf16[2,128,512]{2,1,0:T(8,128)(2,1)S(1)} %collective-permute-done.6.refs_6_), channel_id=1, source_target_pairs={{0,1},{1,0},{2,3},{3,2},{4,5},{5,4},{6,7},{7,6},{8,9},{9,8},{10,11... | collective-permute-start | bytes 786440 | tf_op jit(solution)/shard_map/ppermute | solution.py:233
  20.9 12.4 %collective-permute-start.7 = (bf16[2,128,512]{2,1,0:T(8,128)(2,1)S(1)}, bf16[2,128,512]{2,1,0:T(8,128)(2,1)S(1)}, u32[]{:S(2)}, u32[]{:S(2)}) collective-permute-start(bf16[2,128,512]{2,1,0:T(8,128)(2,1)S(1)} %collective-permute-done.6.refs_6_), channel_id=1, source_target_pairs={{0,2},{1,9},{2,4},{3,11},{4,6},{5,13},{6,0},{7,15},{8,10},{9,17},{... | collective-permute-start | bytes 786440 | tf_op jit(solution)/shard_map/ppermute | solution.py:233
  22.0 11.5 %collective-permute-start.8 = (bf16[2,128,512]{2,1,0:T(8,128)(2,1)S(1)}, bf16[2,128,512]{2,1,0:T(8,128)(2,1)}, u32[]{:S(2)}, u32[]{:S(2)}) collective-permute-start(bf16[2,128,512]{2,1,0:T(8,128)(2,1)S(1)} %collective-permute-done.5.refs_3_), channel_id=1, source_target_pairs={{0,6},{1,25},{2,0},{3,27},{4,2},{5,29},{6,4},{7,31},{8,14},{9,1},{... | collective-permute-start | bytes 786440 | tf_op jit(solution)/shard_map/ppermute | solution.py:233
  27.3 14.8 %all-to-all-start = ((bf16[32,40,128]{2,1,0:T(8,128)(2,1)}), bf16[32,40,128]{2,1,0:T(8,128)(2,1)S(1)}, u32[]{:S(2)}, u32[]{:S(2)}) async-start(bf16[32,40,128]{2,1,0:T(8,128)(2,1)} %bitcast.4), calls=%async_computation | async-start | bytes 655360 | tf_op jit(solution)/shard_map/all_to_all | solution.py:272
  32.3 9.7 %collective-permute-start.12 = (bf16[2,128,512]{2,1,0:T(8,128)(2,1)S(1)}, bf16[2,128,512]{2,1,0:T(8,128)(2,1)}, u32[]{:S(2)}, u32[]{:S(2)}) collective-permute-start(bf16[2,128,512]{2,1,0:T(8,128)(2,1)S(1)} %collective-permute-done.4.refs_2_), channel_id=1, source_target_pairs={{0,1},{1,0},{2,3},{3,2},{4,5},{5,4},{6,7},{7,6},{8,9},{9,8},{10,11... | collective-permute-start | bytes 786440 | tf_op jit(solution)/shard_map/ppermute | solution.py:233
  32.8 9.3 %collective-permute-start.13 = (bf16[2,128,512]{2,1,0:T(8,128)(2,1)S(1)}, bf16[2,128,512]{2,1,0:T(8,128)(2,1)}, u32[]{:S(2)}, u32[]{:S(2)}) collective-permute-start(bf16[2,128,512]{2,1,0:T(8,128)(2,1)S(1)} %collective-permute-done.5.refs_3_), channel_id=1, source_target_pairs={{0,1},{1,0},{2,3},{3,2},{4,5},{5,4},{6,7},{7,6},{8,9},{9,8},{10,11... | collective-permute-start | bytes 786440 | tf_op jit(solution)/shard_map/ppermute | solution.py:233
  32.9 9.1 %collective-permute-start.17 = (bf16[2,128,512]{2,1,0:T(8,128)(2,1)S(1)}, bf16[2,128,512]{2,1,0:T(8,128)(2,1)}, u32[]{:S(2)}, u32[]{:S(2)}) collective-permute-start(bf16[2,128,512]{2,1,0:T(8,128)(2,1)S(1)} %collective-permute-done.9.refs_7_), channel_id=1, source_target_pairs={{0,1},{1,0},{2,3},{3,2},{4,5},{5,4},{6,7},{7,6},{8,9},{9,8},{10,11... | collective-permute-start | bytes 786440 | tf_op jit(solution)/shard_map/ppermute | solution.py:233
  33.3 8.8 %collective-permute-start.14 = (bf16[2,128,512]{2,1,0:T(8,128)(2,1)S(1)}, bf16[2,128,512]{2,1,0:T(8,128)(2,1)}, u32[]{:S(2)}, u32[]{:S(2)}) collective-permute-start(bf16[2,128,512]{2,1,0:T(8,128)(2,1)S(1)} %collective-permute-done.7.refs_4_), channel_id=1, source_target_pairs={{0,1},{1,0},{2,3},{3,2},{4,5},{5,4},{6,7},{7,6},{8,9},{9,8},{10,11... | collective-permute-start | bytes 786440 | tf_op jit(solution)/shard_map/ppermute | solution.py:233
  33.6 8.5 %collective-permute-start.15 = (bf16[2,128,512]{2,1,0:T(8,128)(2,1)}, bf16[2,128,512]{2,1,0:T(8,128)(2,1)}, u32[]{:S(2)}, u32[]{:S(2)}) collective-permute-start(bf16[2,128,512]{2,1,0:T(8,128)(2,1)} %collective-permute-done.8.refs_5_), channel_id=1, source_target_pairs={{0,1},{1,0},{2,3},{3,2},{4,5},{5,4},{6,7},{7,6},{8,9},{9,8},{10,11... | collective-permute-start | bytes 786440 | tf_op jit(solution)/shard_map/ppermute | solution.py:233
  43.4 6.3 %collective-permute-start.18 = (bf16[40,1024]{1,0:T(8,128)(2,1)S(1)}, bf16[40,1024]{1,0:T(8,128)(2,1)S(1)}, u32[]{:S(2)}, u32[]{:S(2)}) collective-permute-start(bf16[40,1024]{1,0:T(8,128)(2,1)S(1)} %shard_map.66), channel_id=1, source_target_pairs={{0,32},{1,33},{2,34},{3,35},{4,36},{5,37},{6,38},{7,39},{8,40},{9,... | collective-permute-start | bytes 245768 | tf_op jit(solution)/shard_map/ppermute | solution.py:279
  50.9 2.8 %collective-permute-start.19 = (bf16[40,1024]{1,0:T(8,128)(2,1)S(1)}, bf16[40,1024]{1,0:T(8,128)(2,1)S(1)}, u32[]{:S(2)}, u32[]{:S(2)}) collective-permute-start(bf16[40,1024]{1,0:T(8,128)(2,1)S(1)} %shard_map.68), channel_id=1, source_target_pairs={{32,64},{33,65},{34,66},{35,67},{36,68},{37,69},{38,70},{39,71},{4... | collective-permute-start | bytes 245768 | tf_op jit(solution)/shard_map/ppermute | solution.py:296
  54.2 0.7 collective-permute-start.20
  55.4 0.7 collective-permute-start.21
  58.9 17.6 %collective-permute-start.24 = (bf16[40,1024]{1,0:T(8,128)(2,1)S(1)}, bf16[40,1024]{1,0:T(8,128)(2,1)S(1)}, u32[]{:S(2)}, u32[]{:S(2)}) collective-permute-start(bf16[40,1024]{1,0:T(8,128)(2,1)S(1)} %fusion.4), channel_id=1, source_target_pairs={{192,224},{193,225},{194,226},{195,227},{196,228},{197,229},{198,2... | collective-permute-start | bytes 245768 | tf_op jit(solution)/shard_map/ppermute | solution.py:305
  (5 other events, 56.2 us)

commit v4 on v3

--- a/solution.py
+++ b/solution.py
@@ -59,26 +59,21 @@
     return jax.ShapeDtypeStruct(dims, dtype)
 
 
-def mask_kernel(mask, starts, refl, own, mask_s, starts_s, refl_v, sems):
-    fetches = [
-        pltpu.make_async_copy(source, target, sems.at[i])
-        for i, (source, target) in enumerate(((refl, refl_v), (mask, mask_s), (starts, starts_s)))
-    ]
+def entry_kernel(mask, starts, refl, panels, own, flip, mask_s, starts_s, refl_v, panels_v, sems):
+    pairs = ((refl, refl_v), (mask, mask_s), (starts, starts_s), (panels, panels_v))
+    fetches = [pltpu.make_async_copy(*pair, sems.at[i]) for i, pair in enumerate(pairs)]
     for fetch in fetches:
         fetch.start()
-    for fetch in fetches:
+    for fetch in fetches[:3]:
         fetch.wait()
     ids = lax.axis_index("row") * SPAN + lax.broadcasted_iota(I32, (SPAN, 128), 0)
     for k in range(WIDTH // 128):
         kept = (ids >= starts_s[0, k]) & (mask_s[0, 0, k] == 1)
         part = refl_v[0, :, k * 128 : (k + 1) * 128].astype(F32)
         own[:, k * 128 : (k + 1) * 128] = jnp.where(kept, part, 0.0).astype(BF)
-
-
-def turn_kernel(panels, out):
-    for k in range(panels.shape[2] // 128):
-        part = panels[0, :, k * 128 : (k + 1) * 128]
-        out[k * 128 : (k + 1) * 128, :] = part.T
+    fetches[3].wait()
+    for k in range(panels_v.shape[2] // 128):
+        flip[k * 128 : (k + 1) * 128, :] = panels_v[0, :, k * 128 : (k + 1) * 128].T
 
 
 def slots(row, sibling):
@@ -256,19 +251,19 @@
     cols = panels.shape[2]
     part = cols // ROWS
 
-    pieces = call(turn_kernel, shape((cols, SPAN)), [VMEM])(panels)
-    own = call(
-        mask_kernel,
-        shape((SPAN, WIDTH)),
-        [HBM] * 3,
+    own, pieces = call(
+        entry_kernel,
+        (shape((SPAN, WIDTH)), shape((cols, SPAN))),
+        [HBM] * 4,
         limit=60,
         scratch=[
             pltpu.SMEM(block_mask.shape, I32),
             pltpu.SMEM(block_starts.shape, I32),
             pltpu.VMEM(reflectors.shape, BF),
-            pltpu.SemaphoreType.DMA((3,)),
+            pltpu.VMEM(panels.shape, BF),
+            pltpu.SemaphoreType.DMA((4,)),
         ],
-    )(block_mask, block_starts, reflectors)
+    )(block_mask, block_starts, reflectors, panels)
     got = lax.all_to_all(pieces.reshape(ROWS, part, SPAN), "row", 0, 0, tiled=True)
     parts = gather_rows(own)
     order, spread = call(

time: 98.1 us -> 96.5 us (0.984)
    pallas_call x2 -> x1, Pallas kernels: 2.57 us -> 1.99 us  [work(): call(entry_kernel, (shape((SPAN, WIDTH)), shape((cols, SPAN))), [HBM] * 4...]
  transfers between devices with their start and end apart: 26 -> 26, of which waited for: 5 -> 5; matrix products, arithmetic and copies ran while one was open for 1% -> 1% of each run, Pallas kernels for 10% -> 9%
where the time goes in v4:
time: 96.5 us; the launch traced here: 96.1 us
  starting transfers between devices  29.1 us (30%)
  waiting for transfers between devices  28.9 us (30%)
  blocking collectives  18 us (19%)
  Pallas kernels  15.6 us (16%)
  matrix products  2.41 us (2%)
  other arithmetic  0.97 us (1%)
    ppermute x18, starting transfers between devices, gather_rows(): pp = lambda value, pairs: lax.ppermute(value, 'row', pairs)  18.8 us
    all_to_all x1, blocking collectives, work(): home = lax.all_to_all(out, 'row', 0, 0, tiled=True)  18 us
    ppermute x5, waiting for transfers between devices, work(): came.append(lax.ppermute(sent, 'front', [(step - 1, step)]))  15.3 us
    all_to_all x1, waiting for transfers between devices, work(): lax.all_to_all(pieces.reshape(ROWS, part, SPAN), 'row', 0, 0, tiled=True)  8.24 us
    pallas_call x1, Pallas kernels, work(): call(base_kernel, (shape((ROWS, SPAN, WIDTH)), shape((part, WIDTH), F32),...  5.66 us
    ppermute x18, waiting for transfers between devices, gather_rows(): pp = lambda value, pairs: lax.ppermute(value, 'row', pairs)  5.4 us
    all_to_all x1, starting transfers between devices, work(): lax.all_to_all(pieces.reshape(ROWS, part, SPAN), 'row', 0, 0, tiled=True)  5.03 us
    ppermute x5, starting transfers between devices, work(): came.append(lax.ppermute(sent, 'front', [(step - 1, step)]))  3.96 us
  transfers between devices with their start and end apart: 26, of which 5 were waited for; matrix products, arithmetic and copies ran while one was open for 1% of the time, Pallas kernels for 9%

profile of v4, /device:TPU:225, one launch (start us, length us, event | category | flops | bytes accessed | tf_op | source)
XLA Modules:
  0.0 96.1 jit_solution(6225131542036600739)
XLA Ops:
  0.0 2.0 %shard_map.64 = (bf16[128,512]{1,0:T(8,128)(2,1)}, bf16[1280,128]{1,0:T(8,128)(2,1)}) custom-call(s32[1,1,4]{2,1,0:T(1,128)} %mask.1, s32[1,4]{1,0:T(1,128)} %starts.1, bf16[1,128,512]{2,1,0:T(8,128)(2,1)} %refl.1, bf16[1,128,1280]{2,1,0:T(8,128)(2,1)} %panels.1), custom_call_target="tpu_custom_call" | custom-call | tf_op jit(solution)/shard_map/pallas_call | solution.py:254
  2.0 1.4 %collective-permute-start.1 = (bf16[128,512]{1,0:T(8,128)(2,1)}, bf16[128,512]{1,0:T(8,128)(2,1)S(1)}, u32[]{:S(2)}, u32[]{:S(2)}) collective-permute-start(bf16[128,512]{1,0:T(8,128)(2,1)} %get-tuple-element.17), channel_id=1, source_target_pairs={{0,8},{1,3},{2,10},{3,5},{4,12},{5,7},{6,14},{7,1},{8,16},{9,11},{... | collective-permute-start | bytes 393224 | tf_op jit(solution)/shard_map/ppermute | solution.py:228
  3.4 1.5 %collective-permute-start = (bf16[128,512]{1,0:T(8,128)(2,1)}, bf16[128,512]{1,0:T(8,128)(2,1)S(1)}, u32[]{:S(2)}, u32[]{:S(2)}) collective-permute-start(bf16[128,512]{1,0:T(8,128)(2,1)} %get-tuple-element.17), channel_id=1, source_target_pairs={{0,24},{1,7},{2,26},{3,1},{4,28},{5,3},{6,30},{7,5},{8,0},{9,15},{... | collective-permute-start | bytes 393224 | tf_op jit(solution)/shard_map/ppermute | solution.py:228
  4.9 2.8 %collective-permute-done.1 = bf16[128,512]{1,0:T(8,128)(2,1)S(1)} collective-permute-done((bf16[128,512]{1,0:T(8,128)(2,1)}, bf16[128,512]{1,0:T(8,128)(2,1)S(1)}, u32[]{:S(2)}, u32[]{:S(2)}) %collective-permute-start.1) | collective-permute-done | bytes 131104 | tf_op jit(solution)/shard_map/ppermute | solution.py:228
  7.7 2.7 %collective-permute-start.3 = (bf16[64,512]{1,0:T(8,128)(2,1)S(1)}, bf16[64,512]{1,0:T(8,128)(2,1)S(1)}, u32[]{:S(2)}, u32[]{:S(2)}) collective-permute-start(bf16[64,512]{1,0:T(8,128)(2,1)S(1)} %slice.9), channel_id=1, source_target_pairs={{0,24},{1,7},{2,26},{3,1},{4,28},{5,3},{6,30},{7,5},{8,0},{9,15},{... | collective-permute-start | bytes 196616 | tf_op jit(solution)/shard_map/ppermute | solution.py:228
  10.5 0.9 pad_maximum_fusion.refs_0_
  11.4 2.1 %collective-permute-start.10 = (bf16[2,128,512]{2,1,0:T(8,128)(2,1)S(1)}, bf16[2,128,512]{2,1,0:T(8,128)(2,1)S(1)}, u32[]{:S(2)}, u32[]{:S(2)}) collective-permute-start(bf16[2,128,512]{2,1,0:T(8,128)(2,1)S(1)} %pad_maximum_fusion.refs_0_), channel_id=1, source_target_pairs={{0,1},{1,0},{2,3},{3,2},{4,5},{5,4},{6,7},{7,6},{8,9},{9,8},{10,11... | collective-permute-start | bytes 786440 | tf_op jit(solution)/shard_map/ppermute | solution.py:228
  13.5 2.7 %collective-permute-start.4 = (bf16[2,128,512]{2,1,0:T(8,128)(2,1)S(1)}, bf16[2,128,512]{2,1,0:T(8,128)(2,1)S(1)}, u32[]{:S(2)}, u32[]{:S(2)}) collective-permute-start(bf16[2,128,512]{2,1,0:T(8,128)(2,1)S(1)} %pad_maximum_fusion.refs_0_), channel_id=1, source_target_pairs={{0,6},{1,25},{2,0},{3,27},{4,2},{5,29},{6,4},{7,31},{8,14},{9,1},{... | collective-permute-start | bytes 786440 | tf_op jit(solution)/shard_map/ppermute | solution.py:228
  16.3 2.4 %collective-permute-start.11 = (bf16[2,128,512]{2,1,0:T(8,128)(2,1)S(1)}, bf16[2,128,512]{2,1,0:T(8,128)(2,1)S(1)}, u32[]{:S(2)}, u32[]{:S(2)}) collective-permute-start(bf16[2,128,512]{2,1,0:T(8,128)(2,1)S(1)} %pad_maximum_fusion.1.refs_1_), channel_id=1, source_target_pairs={{0,1},{1,0},{2,3},{3,2},{4,5},{5,4},{6,7},{7,6},{8,9},{9,8},{10,11... | collective-permute-start | bytes 786440 | tf_op jit(solution)/shard_map/ppermute | solution.py:228
  18.8 1.5 %collective-permute-done.6.refs_6_ = bf16[2,128,512]{2,1,0:T(8,128)(2,1)S(1)} collective-permute-done((bf16[2,128,512]{2,1,0:T(8,128)(2,1)S(1)}, bf16[2,128,512]{2,1,0:T(8,128)(2,1)S(1)}, u32[]{:S(2)}, u32[]{:S(2)}) %collective-permute-start.6) | collective-permute-done | bytes 262176 | tf_op jit(solution)/shard_map/ppermute | solution.py:228
  20.2 0.9 collective-permute-start.16
  21.2 1.1 %collective-permute-done.5.refs_3_ = bf16[2,128,512]{2,1,0:T(8,128)(2,1)S(1)} collective-permute-done((bf16[2,128,512]{2,1,0:T(8,128)(2,1)S(1)}, bf16[2,128,512]{2,1,0:T(8,128)(2,1)S(1)}, u32[]{:S(2)}, u32[]{:S(2)}) %collective-permute-start.5) | collective-permute-done | bytes 262176 | tf_op jit(solution)/shard_map/ppermute | solution.py:228
  22.3 3.4 %collective-permute-start.8 = (bf16[2,128,512]{2,1,0:T(8,128)(2,1)S(1)}, bf16[2,128,512]{2,1,0:T(8,128)(2,1)}, u32[]{:S(2)}, u32[]{:S(2)}) collective-permute-start(bf16[2,128,512]{2,1,0:T(8,128)(2,1)S(1)} %collective-permute-done.5.refs_3_), channel_id=1, source_target_pairs={{0,6},{1,25},{2,0},{3,27},{4,2},{5,29},{6,4},{7,31},{8,14},{9,1},{... | collective-permute-start | bytes 786440 | tf_op jit(solution)/shard_map/ppermute | solution.py:228
  25.7 5.0 %all-to-all-start = ((bf16[32,40,128]{2,1,0:T(8,128)(2,1)}), bf16[32,40,128]{2,1,0:T(8,128)(2,1)S(1)}, u32[]{:S(2)}, u32[]{:S(2)}) async-start(bf16[32,40,128]{2,1,0:T(8,128)(2,1)} %bitcast.21), calls=%async_computation | async-start | bytes 655360 | tf_op jit(solution)/shard_map/all_to_all | solution.py:267
  32.2 8.2 %all-to-all-done.refs_16_.got = bf16[32,40,128]{2,1,0:T(8,128)(2,1)S(1)} async-done(((bf16[32,40,128]{2,1,0:T(8,128)(2,1)}), bf16[32,40,128]{2,1,0:T(8,128)(2,1)S(1)}, u32[]{:S(2)}, u32[]{:S(2)}) %all-to-all-start) | async-done | bytes 327712 | tf_op jit(solution)/shard_map/all_to_all | solution.py:267
  40.5 1.4 %shard_map.65 = bf16[40,1024]{1,0:T(8,128)(2,1)S(1)} custom-call(bf16[2,128,512]{2,1,0:T(8,128)(2,1)S(1)} %pad_maximum_fusion.refs_0_, bf16[2,128,512]{2,1,0:T(8,128)(2,1)S(1)} %pad_maximum_fusion.1.refs_1_, bf16[2,128,512]{2,1,0:T(8,128)(2,1)S(1)} %collective-permute-done.4.refs_2_, bf16[2,128,512]{2,1,0:T(8,128)(2,1)S(1)} %collective-permute-done.5.refs_3_, ...), custom_call_target="tpu_custom_call" | custom-call | tf_op jit(solution)/shard_map/pallas_call | solution.py:273
  42.6 5.7 %shard_map.66 = (bf16[32,128,512]{2,1,0:T(8,128)(2,1)S(1)}, f32[40,512]{1,0:T(8,128)S(1)}, f32[40,1024]{1,0:T(8,128)S(1)}, bf16[1024,512]{1,0:T(8,128)(2,1)S(1)}...) custom-call(bf16[2,128,512]{2,1,0:T(8,128)(2,1)S(1)} %pad_maximum_fusion.refs_0_, ...), custom_call_target="tpu_custom_call" | custom-call | tf_op jit(solution)/shard_map/pallas_call | solution.py:275
  48.2 1.1 %shard_map.67 = bf16[40,1024]{1,0:T(8,128)(2,1)S(1)} custom-call(bf16[40,1024]{1,0:T(8,128)(2,1)S(1)} %collective-permute-done.18.came.c1, f32[40,1024]{1,0:T(8,128)S(1)} %get-tuple-element.19.first, bf16[1024,512]{1,0:T(8,128)(2,1)S(1)} %get-tuple-element.20.gath, bf16[1,512,512]{2,1,0:T(8,128)(2,1)S(1)} %copy-done, ...), custom_call_target="tpu_custom_call" | custom-call | tf_op jit(solution)/shard_map/pallas_call | solution.py:288
  50.0 2.2 %shard_map.68 = (bf16[1024,512]{1,0:T(8,128)(2,1)S(1)}, bf16[1024,1024]{1,0:T(8,128)(2,1)S(1)}) custom-call(s32[1,1024]{1,0:T(1,128)S(1)} %copy-done.1, bf16[1024,512]{1,0:T(8,128)(2,1)S(1)} %get-tuple-element.20.gath, bf16[32,128,512]{2,1,0:T(8,128)(2,1)S(1)} %get-tuple-element.21.eff, bf16[1,512,512]{2,1,0:T(8,128)(2,1)S(1)} %copy-done), custom_call_target="tpu_custom_call" | custom-call | tf_op jit(solution)/shard_map/pallas_call | solution.py:292
  57.4 1.3 %collective-permute-start.24 = (bf16[40,1024]{1,0:T(8,128)(2,1)S(1)}, bf16[40,1024]{1,0:T(8,128)(2,1)S(1)}, u32[]{:S(2)}, u32[]{:S(2)}) collective-permute-start(bf16[40,1024]{1,0:T(8,128)(2,1)S(1)} %fusion.4), channel_id=1, source_target_pairs={{192,224},{193,225},{194,226},{195,227},{196,228},{197,229},{198,2... | collective-permute-start | bytes 245768 | tf_op jit(solution)/shard_map/ppermute | solution.py:300
  58.7 1.0 %shard_map.69 = (bf16[1024,1024]{1,0:T(8,128)(2,1)S(1)}, bf16[1024,1024]{1,0:T(8,128)(2,1)S(1)}) custom-call(s32[1,1024]{1,0:T(1,128)S(1)} %copy-done.1), custom_call_target="tpu_custom_call" | custom-call | tf_op jit(solution)/shard_map/pallas_call | solution.py:269
  59.7 15.2 %collective-permute-done.24.c7 = bf16[40,1024]{1,0:T(8,128)(2,1)S(1)} collective-permute-done((bf16[40,1024]{1,0:T(8,128)(2,1)S(1)}, bf16[40,1024]{1,0:T(8,128)(2,1)S(1)}, u32[]{:S(2)}, u32[]{:S(2)}) %collective-permute-start.24) | collective-permute-done | bytes 81952 | tf_op jit(solution)/shard_map/ppermute | solution.py:300
  74.9 2.3 %shard_map.70 = bf16[32,40,128]{2,1,0:T(8,128)(2,1)S(1)} custom-call(bf16[40,1024]{1,0:T(8,128)(2,1)S(1)} %collective-permute-done.18.came.c1, bf16[40,1024]{1,0:T(8,128)(2,1)S(1)} %collective-permute-done.19.c2, bf16[40,1024]{1,0:T(8,128)(2,1)S(1)} %collective-permute-done.20.c3, bf16[40,1024]{1,0:T(8,128)(2,1)S(1)} %collective-permute-done.21.c4, ...), custom_call_target="tpu_custom_call" | custom-call | tf_op jit(solution)/shard_map/pallas_call | solution.py:302
  77.2 18.0 %all_to_all.10 = bf16[32,40,128]{2,1,0:T(8,128)(2,1)S(1)} all-to-all(bf16[32,40,128]{2,1,0:T(8,128)(2,1)S(1)} %shard_map.70), channel_id=1, replica_groups=mesh['front'=8,'row'=32] {'row'}, dimensions={0} | all-to-all | bytes 655360 | tf_op jit(solution)/shard_map/all_to_all | solution.py:305
  (51 shorter events, 9.0 us)
Async XLA Ops:
  2.0 5.7 %collective-permute-start.1 = (bf16[128,512]{1,0:T(8,128)(2,1)}, bf16[128,512]{1,0:T(8,128)(2,1)S(1)}, u32[]{:S(2)}, u32[]{:S(2)}) collective-permute-start(bf16[128,512]{1,0:T(8,128)(2,1)} %get-tuple-element.17), channel_id=1, source_target_pairs={{0,8},{1,3},{2,10},{3,5},{4,12},{5,7},{6,14},{7,1},{8,16},{9,11},{... | collective-permute-start | bytes 393224 | tf_op jit(solution)/shard_map/ppermute | solution.py:228
  3.4 4.3 %collective-permute-start = (bf16[128,512]{1,0:T(8,128)(2,1)}, bf16[128,512]{1,0:T(8,128)(2,1)S(1)}, u32[]{:S(2)}, u32[]{:S(2)}) collective-permute-start(bf16[128,512]{1,0:T(8,128)(2,1)} %get-tuple-element.17), channel_id=1, source_target_pairs={{0,24},{1,7},{2,26},{3,1},{4,28},{5,3},{6,30},{7,5},{8,0},{9,15},{... | collective-permute-start | bytes 393224 | tf_op jit(solution)/shard_map/ppermute | solution.py:228
  7.7 8.5 %collective-permute-start.2 = (bf16[64,512]{1,0:T(8,128)(2,1)S(1)}, bf16[64,512]{1,0:T(8,128)(2,1)S(1)}, u32[]{:S(2)}, u32[]{:S(2)}) collective-permute-start(bf16[64,512]{1,0:T(8,128)(2,1)S(1)} %slice.8), channel_id=1, source_target_pairs={{0,8},{1,3},{2,10},{3,5},{4,12},{5,7},{6,14},{7,1},{8,16},{9,11},{... | collective-permute-start | bytes 196616 | tf_op jit(solution)/shard_map/ppermute | solution.py:228
  7.7 8.5 %collective-permute-start.3 = (bf16[64,512]{1,0:T(8,128)(2,1)S(1)}, bf16[64,512]{1,0:T(8,128)(2,1)S(1)}, u32[]{:S(2)}, u32[]{:S(2)}) collective-permute-start(bf16[64,512]{1,0:T(8,128)(2,1)S(1)} %slice.9), channel_id=1, source_target_pairs={{0,24},{1,7},{2,26},{3,1},{4,28},{5,3},{6,30},{7,5},{8,0},{9,15},{... | collective-permute-start | bytes 196616 | tf_op jit(solution)/shard_map/ppermute | solution.py:228
  11.4 7.4 %collective-permute-start.10 = (bf16[2,128,512]{2,1,0:T(8,128)(2,1)S(1)}, bf16[2,128,512]{2,1,0:T(8,128)(2,1)S(1)}, u32[]{:S(2)}, u32[]{:S(2)}) collective-permute-start(bf16[2,128,512]{2,1,0:T(8,128)(2,1)S(1)} %pad_maximum_fusion.refs_0_), channel_id=1, source_target_pairs={{0,1},{1,0},{2,3},{3,2},{4,5},{5,4},{6,7},{7,6},{8,9},{9,8},{10,11... | collective-permute-start | bytes 786440 | tf_op jit(solution)/shard_map/ppermute | solution.py:228
  13.5 6.7 %collective-permute-start.6 = (bf16[2,128,512]{2,1,0:T(8,128)(2,1)S(1)}, bf16[2,128,512]{2,1,0:T(8,128)(2,1)S(1)}, u32[]{:S(2)}, u32[]{:S(2)}) collective-permute-start(bf16[2,128,512]{2,1,0:T(8,128)(2,1)S(1)} %pad_maximum_fusion.refs_0_), channel_id=1, source_target_pairs={{0,2},{1,9},{2,4},{3,11},{4,6},{5,13},{6,0},{7,15},{8,10},{9,17},{... | collective-permute-start | bytes 786440 | tf_op jit(solution)/shard_map/ppermute | solution.py:228
  13.5 7.7 %collective-permute-start.4 = (bf16[2,128,512]{2,1,0:T(8,128)(2,1)S(1)}, bf16[2,128,512]{2,1,0:T(8,128)(2,1)S(1)}, u32[]{:S(2)}, u32[]{:S(2)}) collective-permute-start(bf16[2,128,512]{2,1,0:T(8,128)(2,1)S(1)} %pad_maximum_fusion.refs_0_), channel_id=1, source_target_pairs={{0,6},{1,25},{2,0},{3,27},{4,2},{5,29},{6,4},{7,31},{8,14},{9,1},{... | collective-permute-start | bytes 786440 | tf_op jit(solution)/shard_map/ppermute | solution.py:228
  16.2 6.1 %collective-permute-start.5 = (bf16[2,128,512]{2,1,0:T(8,128)(2,1)S(1)}, bf16[2,128,512]{2,1,0:T(8,128)(2,1)S(1)}, u32[]{:S(2)}, u32[]{:S(2)}) collective-permute-start(bf16[2,128,512]{2,1,0:T(8,128)(2,1)S(1)} %pad_maximum_fusion.1.refs_1_), channel_id=1, source_target_pairs={{0,6},{1,25},{2,0},{3,27},{4,2},{5,29},{6,4},{7,31},{8,14},{9,1},{... | collective-permute-start | bytes 786440 | tf_op jit(solution)/shard_map/ppermute | solution.py:228
  16.3 14.4 %collective-permute-start.11 = (bf16[2,128,512]{2,1,0:T(8,128)(2,1)S(1)}, bf16[2,128,512]{2,1,0:T(8,128)(2,1)S(1)}, u32[]{:S(2)}, u32[]{:S(2)}) collective-permute-start(bf16[2,128,512]{2,1,0:T(8,128)(2,1)S(1)} %pad_maximum_fusion.1.refs_1_), channel_id=1, source_target_pairs={{0,1},{1,0},{2,3},{3,2},{4,5},{5,4},{6,7},{7,6},{8,9},{9,8},{10,11... | collective-permute-start | bytes 786440 | tf_op jit(solution)/shard_map/ppermute | solution.py:228
  18.8 12.4 %collective-permute-start.9 = (bf16[2,128,512]{2,1,0:T(8,128)(2,1)S(1)}, bf16[2,128,512]{2,1,0:T(8,128)(2,1)S(1)}, u32[]{:S(2)}, u32[]{:S(2)}) collective-permute-start(bf16[2,128,512]{2,1,0:T(8,128)(2,1)S(1)} %pad_maximum_fusion.1.refs_1_), channel_id=1, source_target_pairs={{0,2},{1,9},{2,4},{3,11},{4,6},{5,13},{6,0},{7,15},{8,10},{9,17},{... | collective-permute-start | bytes 786440 | tf_op jit(solution)/shard_map/ppermute | solution.py:228
  20.2 11.2 %collective-permute-start.16 = (bf16[2,128,512]{2,1,0:T(8,128)(2,1)S(1)}, bf16[2,128,512]{2,1,0:T(8,128)(2,1)S(1)}, u32[]{:S(2)}, u32[]{:S(2)}) collective-permute-start(bf16[2,128,512]{2,1,0:T(8,128)(2,1)S(1)} %collective-permute-done.6.refs_6_), channel_id=1, source_target_pairs={{0,1},{1,0},{2,3},{3,2},{4,5},{5,4},{6,7},{7,6},{8,9},{9,8},{10,11... | collective-permute-start | bytes 786440 | tf_op jit(solution)/shard_map/ppermute | solution.py:228
  21.2 10.6 %collective-permute-start.7 = (bf16[2,128,512]{2,1,0:T(8,128)(2,1)S(1)}, bf16[2,128,512]{2,1,0:T(8,128)(2,1)S(1)}, u32[]{:S(2)}, u32[]{:S(2)}) collective-permute-start(bf16[2,128,512]{2,1,0:T(8,128)(2,1)S(1)} %collective-permute-done.6.refs_6_), channel_id=1, source_target_pairs={{0,2},{1,9},{2,4},{3,11},{4,6},{5,13},{6,0},{7,15},{8,10},{9,17},{... | collective-permute-start | bytes 786440 | tf_op jit(solution)/shard_map/ppermute | solution.py:228
  22.3 9.7 %collective-permute-start.8 = (bf16[2,128,512]{2,1,0:T(8,128)(2,1)S(1)}, bf16[2,128,512]{2,1,0:T(8,128)(2,1)}, u32[]{:S(2)}, u32[]{:S(2)}) collective-permute-start(bf16[2,128,512]{2,1,0:T(8,128)(2,1)S(1)} %collective-permute-done.5.refs_3_), channel_id=1, source_target_pairs={{0,6},{1,25},{2,0},{3,27},{4,2},{5,29},{6,4},{7,31},{8,14},{9,1},{... | collective-permute-start | bytes 786440 | tf_op jit(solution)/shard_map/ppermute | solution.py:228
  25.7 14.8 %all-to-all-start = ((bf16[32,40,128]{2,1,0:T(8,128)(2,1)}), bf16[32,40,128]{2,1,0:T(8,128)(2,1)S(1)}, u32[]{:S(2)}, u32[]{:S(2)}) async-start(bf16[32,40,128]{2,1,0:T(8,128)(2,1)} %bitcast.21), calls=%async_computation | async-start | bytes 655360 | tf_op jit(solution)/shard_map/all_to_all | solution.py:267
  30.8 9.7 %collective-permute-start.12 = (bf16[2,128,512]{2,1,0:T(8,128)(2,1)S(1)}, bf16[2,128,512]{2,1,0:T(8,128)(2,1)}, u32[]{:S(2)}, u32[]{:S(2)}) collective-permute-start(bf16[2,128,512]{2,1,0:T(8,128)(2,1)S(1)} %collective-permute-done.4.refs_2_), channel_id=1, source_target_pairs={{0,1},{1,0},{2,3},{3,2},{4,5},{5,4},{6,7},{7,6},{8,9},{9,8},{10,11... | collective-permute-start | bytes 786440 | tf_op jit(solution)/shard_map/ppermute | solution.py:228
  31.2 9.3 %collective-permute-start.13 = (bf16[2,128,512]{2,1,0:T(8,128)(2,1)S(1)}, bf16[2,128,512]{2,1,0:T(8,128)(2,1)}, u32[]{:S(2)}, u32[]{:S(2)}) collective-permute-start(bf16[2,128,512]{2,1,0:T(8,128)(2,1)S(1)} %collective-permute-done.5.refs_3_), channel_id=1, source_target_pairs={{0,1},{1,0},{2,3},{3,2},{4,5},{5,4},{6,7},{7,6},{8,9},{9,8},{10,11... | collective-permute-start | bytes 786440 | tf_op jit(solution)/shard_map/ppermute | solution.py:228
  31.4 9.1 %collective-permute-start.17 = (bf16[2,128,512]{2,1,0:T(8,128)(2,1)S(1)}, bf16[2,128,512]{2,1,0:T(8,128)(2,1)}, u32[]{:S(2)}, u32[]{:S(2)}) collective-permute-start(bf16[2,128,512]{2,1,0:T(8,128)(2,1)S(1)} %collective-permute-done.9.refs_7_), channel_id=1, source_target_pairs={{0,1},{1,0},{2,3},{3,2},{4,5},{5,4},{6,7},{7,6},{8,9},{9,8},{10,11... | collective-permute-start | bytes 786440 | tf_op jit(solution)/shard_map/ppermute | solution.py:228
  31.7 8.8 %collective-permute-start.14 = (bf16[2,128,512]{2,1,0:T(8,128)(2,1)S(1)}, bf16[2,128,512]{2,1,0:T(8,128)(2,1)}, u32[]{:S(2)}, u32[]{:S(2)}) collective-permute-start(bf16[2,128,512]{2,1,0:T(8,128)(2,1)S(1)} %collective-permute-done.7.refs_4_), channel_id=1, source_target_pairs={{0,1},{1,0},{2,3},{3,2},{4,5},{5,4},{6,7},{7,6},{8,9},{9,8},{10,11... | collective-permute-start | bytes 786440 | tf_op jit(solution)/shard_map/ppermute | solution.py:228
  32.0 8.5 %collective-permute-start.15 = (bf16[2,128,512]{2,1,0:T(8,128)(2,1)}, bf16[2,128,512]{2,1,0:T(8,128)(2,1)}, u32[]{:S(2)}, u32[]{:S(2)}) collective-permute-start(bf16[2,128,512]{2,1,0:T(8,128)(2,1)} %collective-permute-done.8.refs_5_), channel_id=1, source_target_pairs={{0,1},{1,0},{2,3},{3,2},{4,5},{5,4},{6,7},{7,6},{8,9},{9,8},{10,11... | collective-permute-start | bytes 786440 | tf_op jit(solution)/shard_map/ppermute | solution.py:228
  41.9 6.3 %collective-permute-start.18 = (bf16[40,1024]{1,0:T(8,128)(2,1)S(1)}, bf16[40,1024]{1,0:T(8,128)(2,1)S(1)}, u32[]{:S(2)}, u32[]{:S(2)}) collective-permute-start(bf16[40,1024]{1,0:T(8,128)(2,1)S(1)} %shard_map.65), channel_id=1, source_target_pairs={{0,32},{1,33},{2,34},{3,35},{4,36},{5,37},{6,38},{7,39},{8,40},{9,... | collective-permute-start | bytes 245768 | tf_op jit(solution)/shard_map/ppermute | solution.py:274
  49.3 2.8 %collective-permute-start.19 = (bf16[40,1024]{1,0:T(8,128)(2,1)S(1)}, bf16[40,1024]{1,0:T(8,128)(2,1)S(1)}, u32[]{:S(2)}, u32[]{:S(2)}) collective-permute-start(bf16[40,1024]{1,0:T(8,128)(2,1)S(1)} %shard_map.67), channel_id=1, source_target_pairs={{32,64},{33,65},{34,66},{35,67},{36,68},{37,69},{38,70},{39,71},{4... | collective-permute-start | bytes 245768 | tf_op jit(solution)/shard_map/ppermute | solution.py:291
  52.7 0.7 collective-permute-start.20
  55.0 0.7 collective-permute-start.22
  57.4 17.6 %collective-permute-start.24 = (bf16[40,1024]{1,0:T(8,128)(2,1)S(1)}, bf16[40,1024]{1,0:T(8,128)(2,1)S(1)}, u32[]{:S(2)}, u32[]{:S(2)}) collective-permute-start(bf16[40,1024]{1,0:T(8,128)(2,1)S(1)} %fusion.4), channel_id=1, source_target_pairs={{192,224},{193,225},{194,226},{195,227},{196,228},{197,229},{198,2... | collective-permute-start | bytes 245768 | tf_op jit(solution)/shard_map/ppermute | solution.py:300
  (4 other events, 53.7 us)
